TPU v7x, 32 devices: a whole 2x2x4 slice. The times are simulated.
32 devices in a mesh: fsdp: 8 (over z, x), rep: 4 (over y, core).
Axes of the slice: x: 2, y: 2, z: 4, core: 2. Of those that a mesh axis runs over, the one named last changes fastest.
Arguments:
- samples: bfloat16 [768, 4096], P(('fsdp', 'rep')), may hold values from -10 to 10
- dual_weight: bfloat16 [8192, 4096], P('fsdp'), may hold values from -0.09375 to 0.09375
- dual_vector: float32 [2, 8192], P(None, 'fsdp'), may hold values from 0 to 2
- map_weight: float32 [8192, 4096], P(('fsdp', 'rep')), may hold values from -0.09375 to 0.09375
- map_vector: float32 [2, 8192], P(None, ('fsdp', 'rep')), may hold values from 0.001 to 2
- moment_weight: float32 [8192, 4096], P(('fsdp', 'rep')), may hold values from -0.006 to 0.006
- square_weight: float32 [8192, 4096], P(('fsdp', 'rep')), may hold values from 0.0001 to 0.01
- moment_vector: float32 [2, 8192], P(None, ('fsdp', 'rep')), may hold values from -0.03 to 0.03
- square_vector: float32 [2, 8192], P(None, ('fsdp', 'rep')), may hold values from 0.0001 to 0.01
Outputs:
- next_weight: float32 [8192, 4096], P(('fsdp', 'rep'))
- next_vector: float32 [2, 8192], P(None, ('fsdp', 'rep'))
- next_moment_weight: float32 [8192, 4096], P(('fsdp', 'rep'))
- next_square_weight: float32 [8192, 4096], P(('fsdp', 'rep'))
- next_moment_vector: float32 [2, 8192], P(None, ('fsdp', 'rep'))
- next_square_vector: float32 [2, 8192], P(None, ('fsdp', 'rep'))
All inputs are finite; a program needn't handle non-finite values.
Results may differ from a plain program's by a relative error of at most 0.004.
Values may be sent and summed in bfloat16 or wider, within the bound.
A program may use at most 128 MiB of HBM per device.

v0:
```python
import jax
import jax.numpy as jnp
from jax import lax
from jax.sharding import PartitionSpec as P

beta_one = 0.9
beta_two = 0.999
learn_rate = 0.001
epsilon = 1e-08
adam_step = 10


def contract_last(left, right):
    return lax.dot_general(
        left, right, (((1,), (1,)), ((), ())), preferred_element_type=jnp.float32
    )


def contract_first(left, right):
    return lax.dot_general(
        left, right, (((0,), (0,)), ((), ())), preferred_element_type=jnp.float32
    )


def adam_update(param, grad, moment, square):
    moment_new = beta_one * moment + (1.0 - beta_one) * grad
    square_new = beta_two * square + (1.0 - beta_two) * grad * grad
    fix_one = 1.0 - beta_one**adam_step
    fix_two = 1.0 - beta_two**adam_step
    update = learn_rate * (moment_new / fix_one) / (jnp.sqrt(square_new / fix_two) + epsilon)
    return (param - update, moment_new, square_new)


def body(
    samples,
    dual_weight,
    dual_vector,
    map_weight,
    map_vector,
    moment_weight,
    square_weight,
    moment_vector,
    square_vector,
):
    group_rows = lax.all_gather(samples, "fsdp", axis=0, tiled=True)
    weight_slab, vector_slab = (
        lax.all_gather(map_weight.astype(jnp.bfloat16), "rep", axis=0, tiled=True),
        lax.all_gather(map_vector.astype(jnp.bfloat16), "rep", axis=1, tiled=True),
    )
    readout = vector_slab[0].astype(jnp.float32)
    offset = vector_slab[1].astype(jnp.float32)
    inverse_rows = 1.0 / (group_rows.shape[0] * lax.axis_size("rep"))
    hidden = contract_last(group_rows, weight_slab) + offset
    sigma = jax.nn.sigmoid(hidden)
    scaled = (readout * sigma).astype(jnp.bfloat16)
    group_float = group_rows.astype(jnp.float32)
    mapped = group_float + lax.psum(
        jnp.dot(scaled, weight_slab, preferred_element_type=jnp.float32).astype(jnp.bfloat16),
        "fsdp",
    ).astype(jnp.float32)
    mapped_low = mapped.astype(jnp.bfloat16)
    dual_hidden = contract_last(mapped_low, dual_weight) + dual_vector[1]
    dual_scaled = (dual_vector[0] * jax.nn.sigmoid(dual_hidden)).astype(jnp.bfloat16)
    dual_grad = mapped + lax.psum(
        jnp.dot(dual_scaled, dual_weight, preferred_element_type=jnp.float32).astype(jnp.bfloat16),
        "fsdp",
    ).astype(jnp.float32)
    residual = (group_float - dual_grad).astype(jnp.bfloat16)
    pulled = contract_last(residual, weight_slab)
    slope = sigma * (1.0 - sigma)
    curve_float = readout * slope * pulled
    curve_term = curve_float.astype(jnp.bfloat16)
    left_stack = jnp.concatenate([scaled, curve_term], axis=0)
    right_stack = jnp.concatenate([residual, group_rows], axis=0)
    grad_slab = contract_first(left_stack, right_stack) * inverse_rows
    grad_small = (
        jnp.stack([jnp.sum(sigma * pulled, axis=0), jnp.sum(curve_float, axis=0)]) * inverse_rows
    )
    owner_weight, owner_vector = (
        lax.psum_scatter(grad_slab, "rep", scatter_dimension=0, tiled=True),
        lax.psum_scatter(grad_small, "rep", scatter_dimension=1, tiled=True),
    )
    next_weight, next_moment_weight, next_square_weight = adam_update(
        map_weight, owner_weight, moment_weight, square_weight
    )
    raw_vector, next_moment_vector, next_square_vector = adam_update(
        map_vector, owner_vector, moment_vector, square_vector
    )
    next_vector = jnp.concatenate([jnp.maximum(raw_vector[0:1], 0.0), raw_vector[1:2]], axis=0)
    return (
        next_weight,
        next_vector,
        next_moment_weight,
        next_square_weight,
        next_moment_vector,
        next_square_vector,
    )


def solution(mesh):
    return jax.shard_map(
        body,
        mesh=mesh,
        in_specs=(
            P(("fsdp", "rep"), None),
            P("fsdp", None),
            P(None, "fsdp"),
            P(("fsdp", "rep"), None),
            P(None, ("fsdp", "rep")),
            P(("fsdp", "rep"), None),
            P(("fsdp", "rep"), None),
            P(None, ("fsdp", "rep")),
            P(None, ("fsdp", "rep")),
        ),
        out_specs=(
            P(("fsdp", "rep"), None),
            P(None, ("fsdp", "rep")),
            P(("fsdp", "rep"), None),
            P(("fsdp", "rep"), None),
            P(None, ("fsdp", "rep")),
            P(None, ("fsdp", "rep")),
        ),
        check_vma=False,
    )
```

profile of v0, /device:TPU:17, one launch (start us, length us, event | category | flops | bytes accessed | tf_op | source)
XLA Modules:
  0.0 492.9 jit_solution(3073785880574631769)
XLA Ops:
  7.2 0.0 all-gather.3.cloned.1.call-start
  7.2 0.7 all-gather.3.cloned.1.call-update
  7.9 0.0 copy-start.1
  7.9 0.0 all-gather.5.cloned.1.call-start
  8.0 3.8 convert_element_type.41
  11.8 0.0 all-gather.5.cloned.1.call-update
  11.8 0.0 all-reduce.3.cloned.1.call-start
  11.8 0.0 copy-done.1
  11.8 5.6 %all_gather.9 = bf16[2,1024]{1,0:T(2,128)(2,1)S(1)} all-gather(bf16[2,256]{1,0:T(2,128)(2,1)S(1)} %convert_element_type.40), channel_id=1, replica_groups=mesh['fsdp'=8,'rep'=4] {'rep'}, dimensions={1}, use_global_device_ids=true | all-gather | bytes 5120 | tf_op jit(solution)/shard_map/all_gather | solution.py:48
  17.4 36.4 %all-gather.3.cloned.1.call-done = bf16[192,4096]{1,0:T(8,128)(2,1)} async-done(((bf16[24,4096]{1,0:T(8,128)(2,1)}), bf16[192,4096]{1,0:T(8,128)(2,1)}) %all-gather.3.cloned.1.call-update) | async-done | bytes 1572880 | tf_op jit(solution)/shard_map/all_gather | solution.py:45
  53.8 60.9 %all-gather.5.cloned.1.call-done = bf16[1024,4096]{1,0:T(8,128)(2,1)} async-done(((bf16[256,4096]{1,0:T(8,128)(2,1)}), bf16[1024,4096]{1,0:T(8,128)(2,1)}) %all-gather.5.cloned.1.call-update) | async-done | bytes 8388624 | tf_op jit(solution)/shard_map/all_gather | solution.py:47
  114.6 0.0 copy-start.5
  114.7 7.9 %multiply_convert_fusion = (bf16[192,1024]{1,0:T(8,128)(2,1)S(1)}, f32[192,1024]{1,0:T(8,128)}) fusion(f32[1024]{0:T(1024)S(1)} %bitcast.18, f32[1024]{0:T(1024)S(1)} %bitcast.20, bf16[192,4096]{1,0:T(8,128)(2,1)} %all-gather.3.cloned.1.call-done, bf16[1024,4096]{1,0:T(8,128)(2,1)} %all-gather.5.cloned.1.call-done), kind=kOutput, calls=%fused_computation.34 | convolution fusion | flops 1611792384 | bytes 11149312 | tf_op jit(solution)/shard_map/dot_general | solution.py:14
  122.5 0.0 copy-done.5
  122.5 0.0 copy-start.2
  122.5 0.0 copy-start
  122.5 3.0 convolution_convert_fusion.1
  125.5 0.0 all-reduce.3.cloned.1.call-update
  125.6 0.0 all-reduce.5.cloned.1.call-start
  125.6 0.0 copy-done.2
  125.6 87.8 %all-reduce.3.cloned.1.call-done = bf16[192,4096]{1,0:T(8,128)(2,1)} async-done(((bf16[192,4096]{1,0:T(8,128)(2,1)}), bf16[192,4096]{1,0:T(8,128)(2,1)}) %all-reduce.3.cloned.1.call-update) | async-done | bytes 1572880 | tf_op jit(solution)/shard_map/psum | solution.py:57
  213.4 0.0 copy-done
  213.4 12.0 %convolution_convert_fusion = bf16[192,4096]{1,0:T(8,128)(2,1)} fusion(bf16[1024,4096]{1,0:T(8,128)(2,1)} %param.10, bf16[192,4096]{1,0:T(8,128)(2,1)} %all-reduce.3.cloned.1.call-done, bf16[192,4096]{1,0:T(8,128)(2,1)S(1)} %copy-done, f32[1024]{0:T(1024)S(1)} %bitcast.22, f32[1024]{0:T(1024)S(1)} %bitcast.21), kind=kOutput, calls=%fused_computation.2 | convolution fusion | flops 3226337280 | bytes 13115392 | tf_op jit(solution)/shard_map/dot_general | solution.py:65
  225.4 0.0 all-reduce.5.cloned.1.call-update
  225.4 0.0 reduce-scatter.7.cloned.1.call-start
  225.4 88.6 %all-reduce.5.cloned.1.call-done = bf16[192,4096]{1,0:T(8,128)(2,1)} async-done(((bf16[192,4096]{1,0:T(8,128)(2,1)}), bf16[192,4096]{1,0:T(8,128)(2,1)}) %all-reduce.5.cloned.1.call-update) | async-done | bytes 1572880 | tf_op jit(solution)/shard_map/psum | solution.py:64
  314.1 2.7 fusion.1
  316.8 7.2 %multiply_reduce_fusion = (f32[1024]{0:T(1024)S(1)}, f32[1024]{0:T(1024)S(1)}, bf16[192,1024]{1,0:T(8,128)(2,1)}) fusion(f32[192,1024]{1,0:T(8,128)} %get-tuple-element.22, f32[1024]{0:T(1024)S(1)} %bitcast.19, bf16[192,4096]{1,0:T(8,128)(2,1)S(1)} %fusion.1, bf16[1024,4096]{1,0:T(8,128)(2,1)} %all-gather.5.cloned.1.call-done), kind=kOutput, calls=%fused_computation.33 | convolution fusion | flops 1612183552 | bytes 11153408 | tf_op jit(solution)/shard_map/dot_general | solution.py:14
  324.0 1.0 copy.15
  325.1 0.0 reduce-scatter.7.cloned.1.call-update
  325.1 0.2 reduce-scatter.5.cloned.1.call-start
  325.3 9.3 %convolution_multiply_fusion = f32[1024,4096]{1,0:T(8,128)} fusion(bf16[192,4096]{1,0:T(8,128)(2,1)S(1)} %copy-done, bf16[192,4096]{1,0:T(8,128)(2,1)S(1)} %fusion.1, bf16[192,1024]{1,0:T(8,128)(2,1)} %get-tuple-element.14, bf16[192,1024]{1,0:T(8,128)(2,1)S(1)} %get-tuple-element.21), kind=kOutput, calls=%fused_computation | convolution fusion | flops 3233284096 | bytes 20709376 | tf_op jit(solution)/shard_map/dot_general | solution.py:20
  334.6 0.0 copy-start.3
  334.6 0.0 copy-start.4
  334.6 0.0 reduce-scatter.5.cloned.1.call-update
  334.6 12.5 %reduce-scatter.7.cloned.1.call-done = f32[256,2]{1,0:T(8,128)} async-done(((f32[1024,2]{1,0:T(8,128)}), f32[256,2]{1,0:T(8,128)}) %reduce-scatter.7.cloned.1.call-update) | async-done | bytes 2064
  347.2 1.0 copy.16
  348.1 0.0 copy-done.3
  348.1 0.0 copy-done.4
  348.2 0.6 divide_subtract_fusion.1
  348.8 0.6 pad_maximum_fusion
  349.3 125.3 %reduce-scatter.5.cloned.1.call-done = f32[256,4096]{1,0:T(8,128)} async-done(((f32[1024,4096]{1,0:T(8,128)}), f32[256,4096]{1,0:T(8,128)}) %reduce-scatter.5.cloned.1.call-update) | async-done | bytes 4194320 | tf_op jit(solution)/shard_map/reduce_scatter | solution.py:80
  474.7 11.4 %divide_subtract_fusion = (f32[256,4096]{1,0:T(8,128)}, f32[256,4096]{1,0:T(8,128)}, f32[256,4096]{1,0:T(8,128)}) fusion(f32[256,4096]{1,0:T(8,128)} %param.12, f32[256,4096]{1,0:T(8,128)} %reduce-scatter.5.cloned.1.call-done, f32[256,4096]{1,0:T(8,128)} %param.14, f32[256,4096]{1,0:T(8,128)} %param.15), kind=kLoop, calls=%fused_computation.5 | loop fusion | flops 12582912 | bytes 29360128 | tf_op jit(solution)/shard_map/sub | solution.py:31
  (5 shorter events, 0.0 us)
Async XLA Ops:
  7.2 46.6 %all-gather.3.cloned.1.call-start = ((), (), s32[]{:S(2)}) async-start(), calls=%async_computation.2 | async-start | bytes 1769472 | tf_op jit(solution)/shard_map/all_gather | solution.py:45
  7.9 3.9 copy-start.1
  7.9 106.7 %all-gather.5.cloned.1.call-start = ((), (), s32[]{:S(2)}) async-start(), calls=%async_computation.3 | async-start | bytes 10485760 | tf_op jit(solution)/shard_map/all_gather | solution.py:47
  11.8 201.6 %all-reduce.3.cloned.1.call-start = ((), (), s32[]{:S(2)}) async-start(), calls=%async_computation.4 | async-start | bytes 3145728 | tf_op jit(solution)/shard_map/psum | solution.py:57
  114.6 7.9 %copy-start.5 = (bf16[1024,4096]{1,0:T(8,128)(2,1)S(1)}, bf16[1024,4096]{1,0:T(8,128)(2,1)}, u32[]{:S(2)}) copy-start(bf16[1024,4096]{1,0:T(8,128)(2,1)} %all-gather.5.cloned.1.call-done) | copy-start | bytes 25165828
  122.5 3.1 copy-start.2
  122.5 90.9 %copy-start = (bf16[192,4096]{1,0:T(8,128)(2,1)S(1)}, bf16[192,4096]{1,0:T(8,128)(2,1)}, u32[]{:S(2)}) copy-start(bf16[192,4096]{1,0:T(8,128)(2,1)} %all-gather.3.cloned.1.call-done) | copy-start | bytes 4718596
  125.6 188.5 %all-reduce.5.cloned.1.call-start = ((), (), s32[]{:S(2)}) async-start(), calls=%async_computation.5 | async-start | bytes 3145728 | tf_op jit(solution)/shard_map/psum | solution.py:64
  225.4 121.8 %reduce-scatter.7.cloned.1.call-start = ((), (), s32[]{:S(2)}) async-start(), calls=%async_computation.7 | async-start | bytes 655360
  325.1 149.6 %reduce-scatter.5.cloned.1.call-start = ((), (), s32[]{:S(2)}) async-start(), calls=%async_computation.6 | async-start | bytes 20971520 | tf_op jit(solution)/shard_map/reduce_scatter | solution.py:80
  334.6 13.5 %copy-start.3 = (f32[2,256]{1,0:T(2,128)S(1)}, f32[2,256]{1,0:T(2,128)}, u32[]{:S(2)}) copy-start(f32[2,256]{1,0:T(2,128)} %param.16) | copy-start | bytes 6148
  334.6 13.5 %copy-start.4 = (f32[2,256]{1,0:T(2,128)S(1)}, f32[2,256]{1,0:T(2,128)}, u32[]{:S(2)}) copy-start(f32[2,256]{1,0:T(2,128)} %param.17) | copy-start | bytes 6148
Sparse Core Ops, SparseCore 0:
  10.2 43.5 all-gather.2
  55.9 58.6 all-gather.4
  125.7 87.6 all-reduce.2
  225.5 88.5 all-reduce.4
  325.2 21.9 reduce-scatter.6
  349.6 125.0 reduce-scatter.4
where the time goes:
time: 495 us; the launch traced here: 493 us
  waiting for transfers between devices  412 us (83%)
  matrix products  39.4 us (8%)
  other arithmetic  19.1 us (4%)
  between operations  14.2 us (3%)
  blocking collectives  5.58 us (1%)
    reduce_scatter x1, waiting for transfers between devices, body(): lax.psum_scatter(grad_slab, 'rep', scatter_dimension=0, tiled=True)  125 us
    psum x1, waiting for transfers between devices, body(): lax.psum(jnp.dot(dual_scaled, dual_weight, preferred_element_type=jnp.flo...  88.6 us
    psum x1, waiting for transfers between devices, body(): lax.psum(jnp.dot(scaled, weight_slab, preferred_element_type=jnp.float32)...  87.8 us
    all_gather x1, waiting for transfers between devices, body(): lax.all_gather(map_weight.astype(jnp.bfloat16), 'rep', axis=0, tiled=True)  60.9 us
    all_gather x1, waiting for transfers between devices, body(): group_rows = lax.all_gather(samples, 'fsdp', axis=0, tiled=True)  36.4 us
    dot_general x2, matrix products, contract_last(): lax.dot_general(left, right, (((1,), (1,)), ((), ())), preferred_element_...  15.1 us
    unnamed x7, waiting for transfers between devices  13.3 us
    sub x2, other arithmetic, adam_update(): return (param - update, moment_new, square_new)  12 us
  transfers between devices with their start and end apart: 6, of which 6 were waited for; matrix products, arithmetic and copies ran while one was open for 3% of the time, Pallas kernels for 0%

commit v1 on v0

--- a/solution.py
+++ b/solution.py
@@ -1,6 +1,8 @@
 import jax
 import jax.numpy as jnp
 from jax import lax
+from jax.experimental import pallas as pl
+from jax.experimental.pallas import tpu as pltpu
 from jax.sharding import PartitionSpec as P
 
 beta_one = 0.9
@@ -29,6 +31,320 @@
     fix_two = 1.0 - beta_two**adam_step
     update = learn_rate * (moment_new / fix_one) / (jnp.sqrt(square_new / fix_two) + epsilon)
     return (param - update, moment_new, square_new)
+
+
+MESH = pl.DeviceIdType.MESH
+F32 = jnp.float32
+BF16 = jnp.bfloat16
+
+
+def place():
+    fsdp, rep = lax.axis_index("fsdp"), lax.axis_index("rep")
+    z, x = fsdp // 2, fsdp % 2
+    y, core = rep // 2, rep % 2
+    z_peers = [(lax.rem(z + k, 4) * 2 + x, rep) for k in (1, 2, 3)]
+    x_peer = (z * 2 + 1 - x, rep)
+    y_peer = (fsdp, (1 - y) * 2 + core)
+    return z, x, y, z_peers, x_peer, y_peer
+
+
+def greet(peers):
+    barrier = pltpu.get_barrier_semaphore()
+    for peer in peers:
+        pl.semaphore_signal(barrier, inc=1, device_id=peer, device_id_type=MESH)
+    pl.semaphore_wait(barrier, len(peers))
+
+
+class Sender:
+    def __init__(self, send_sem, recv_sem):
+        self.send_sem, self.recv_sem, self.copies = send_sem, recv_sem, []
+
+    def send(self, src, dst, device):
+        i = len(self.copies)
+        copy = pltpu.make_async_remote_copy(
+            src_ref=src,
+            dst_ref=dst,
+            send_sem=self.send_sem.at[i],
+            recv_sem=self.recv_sem.at[i],
+            device_id=device,
+            device_id_type=MESH,
+        )
+        copy.start()
+        self.copies.append(copy)
+        return copy
+
+    def drain(self):
+        for copy in self.copies:
+            copy.wait_send()
+
+
+def gather_line(sender, view, z, x, y, z_peers, x_peer, y_peer, own):
+    here = view(z, x, y)
+    to_z = [sender.send(own, here, peer) for peer in z_peers]
+    over_x, over_y = [sender.send(own, here, x_peer)], []
+    if y_peer is not None:
+        over_y.append(sender.send(own, here, y_peer))
+    for k in (1, 3, 2):
+        source = lax.rem(z + 4 - k, 4)
+        to_z[k - 1].wait_recv()
+        block = view(source, x, y)
+        over_x.append(sender.send(block, block, x_peer))
+        if y_peer is not None:
+            over_y.append(sender.send(block, block, y_peer))
+    return over_x, over_y
+
+
+def gather_all(sender, view, half, z, x, y, z_peers, x_peer, y_peer, own):
+    over_x, over_y = gather_line(sender, view, z, x, y, z_peers, x_peer, y_peer, own)
+    diagonal = []
+    for i, k in enumerate((0, 1, 3, 2)):
+        source = lax.rem(z + 4 - k, 4)
+        over_x[i].wait_recv()
+        block = half(source, 1 - x, y, 0)
+        diagonal.append(sender.send(block, block, y_peer))
+        over_y[i].wait_recv()
+        block = half(source, x, 1 - y, 1)
+        diagonal.append(sender.send(block, block, x_peer))
+    for copy in diagonal:
+        copy.wait_recv()
+
+
+def gather_kernel(own_ref, all_ref, send_sem, recv_sem, local_sem):
+    z, x, y, z_peers, x_peer, y_peer = place()
+    width = own_ref.shape[1] // 2
+    view = lambda zz, xx, yy: all_ref.at[yy * 8 + zz * 2 + xx]
+    half = lambda zz, xx, yy, h: all_ref.at[yy * 8 + zz * 2 + xx, :, pl.ds(h * width, width)]
+    greet(z_peers + [x_peer, y_peer])
+    local = pltpu.make_async_copy(own_ref, view(z, x, y), local_sem)
+    local.start()
+    sender = Sender(send_sem, recv_sem)
+    gather_all(sender, view, half, z, x, y, z_peers, x_peer, y_peer, own_ref)
+    sender.drain()
+    local.wait()
+
+
+def gather_samples(samples):
+    rows, width = samples.shape
+    gathered = pl.pallas_call(
+        gather_kernel,
+        out_shape=jax.ShapeDtypeStruct((16, rows, width), samples.dtype),
+        in_specs=[pl.BlockSpec(memory_space=pl.ANY)],
+        out_specs=pl.BlockSpec(memory_space=pl.ANY),
+        scratch_shapes=[
+            pltpu.SemaphoreType.DMA((19,)),
+            pltpu.SemaphoreType.DMA((19,)),
+            pltpu.SemaphoreType.DMA,
+        ],
+        compiler_params=pltpu.CompilerParams(collective_id=1, has_side_effects=True),
+        cost_estimate=pl.CostEstimate(flops=0, bytes_accessed=100_000_000, transcendentals=0),
+    )(samples)
+    return gathered.reshape(16 * rows, width)
+
+
+def map_kernel(
+    part, base, mapped, low, from_y, from_x, to_x, to_y, late_x, late_y, to_z, from_z, send_sem, recv_sem
+):
+    z, x, y, z_peers, x_peer, y_peer = place()
+    rows, width = base.shape
+    half = rows // 2
+    cols = lambda zz, xx: pl.ds(pl.multiple_of((zz * 2 + xx) * width, width), width)
+    lines = lambda yy, h: pl.ds(pl.multiple_of(yy * rows + h * half, half), half)
+    lane = lambda xx: pl.ds(pl.multiple_of(xx * width, width), width)
+    greet(z_peers + [x_peer, y_peer])
+    sender = Sender(send_sem, recv_sem)
+    order = (2, 1, 3, 0)
+    first_y, first_x = {}, {}
+    for k in order:
+        zz = lax.rem(z + k, 4)
+        pair = pl.ds(pl.multiple_of(zz * 2 * width, 2 * width), 2 * width)
+        first_y[k] = sender.send(part.at[lines(1 - y, 0), pair], from_y.at[k], y_peer)
+        first_x[k] = [
+            sender.send(part.at[lines(yy, 1), cols(zz, 1 - x)], from_x.at[k, yy], x_peer) for yy in (0, 1)
+        ]
+    second_x, second_y = {}, {}
+    for k in order:
+        zz = lax.rem(z + k, 4)
+        first_y[k].wait_recv()
+        to_x[k] = (
+            part[lines(y, 0), cols(zz, 1 - x)].astype(F32) + from_y[k, :, lane(1 - x)].astype(F32)
+        ).astype(BF16)
+        second_x[k] = sender.send(to_x.at[k], late_x.at[k], x_peer)
+        for copy in first_x[k]:
+            copy.wait_recv()
+        to_y[k] = (
+            part[lines(1 - y, 1), cols(zz, x)].astype(F32) + from_x[k, 1 - y].astype(F32)
+        ).astype(BF16)
+        second_y[k] = sender.send(to_y.at[k], late_y.at[k], y_peer)
+    third = {}
+    for k in order:
+        zz = lax.rem(z + k, 4)
+        second_x[k].wait_recv()
+        top = (
+            part[lines(y, 0), cols(zz, x)].astype(F32)
+            + from_y[k, :, lane(x)].astype(F32)
+            + late_x[k].astype(F32)
+        )
+        second_y[k].wait_recv()
+        bottom = (
+            part[lines(y, 1), cols(zz, x)].astype(F32) + from_x[k, y].astype(F32) + late_y[k].astype(F32)
+        )
+        if k:
+            to_z[k - 1, :half] = top.astype(BF16)
+            to_z[k - 1, half:] = bottom.astype(BF16)
+            third[k] = sender.send(to_z.at[k - 1], from_z.at[k - 1], z_peers[k - 1])
+        else:
+            mapped[:half] = top + base[:half].astype(F32)
+            mapped[half:] = bottom + base[half:].astype(F32)
+    for k in (1, 2, 3):
+        third[k].wait_recv()
+    total = mapped[...] + (from_z[0].astype(F32) + from_z[1].astype(F32) + from_z[2].astype(F32))
+    mapped[...] = total
+    low[:, cols(z, x)] = total.astype(BF16)
+    view = lambda zz, xx, yy: low.at[:, cols(zz, xx)]
+    over_x, _ = gather_line(sender, view, z, x, y, z_peers, x_peer, None, view(z, x, y))
+    for copy in over_x:
+        copy.wait_recv()
+    sender.drain()
+
+
+def reduce_map(part, base):
+    rows, width = base.shape
+    half = rows // 2
+    return pl.pallas_call(
+        map_kernel,
+        out_shape=(
+            jax.ShapeDtypeStruct((rows, width), F32),
+            jax.ShapeDtypeStruct((rows, part.shape[1]), BF16),
+        ),
+        in_specs=[pl.BlockSpec(memory_space=pltpu.VMEM)] * 2,
+        out_specs=[pl.BlockSpec(memory_space=pltpu.VMEM)] * 2,
+        scratch_shapes=[
+            pltpu.VMEM((4, half, 2 * width), BF16),
+            pltpu.VMEM((4, 2, half, width), BF16),
+            pltpu.VMEM((4, half, width), BF16),
+            pltpu.VMEM((4, half, width), BF16),
+            pltpu.VMEM((4, half, width), BF16),
+            pltpu.VMEM((4, half, width), BF16),
+            pltpu.VMEM((3, rows, width), BF16),
+            pltpu.VMEM((3, rows, width), BF16),
+            pltpu.SemaphoreType.DMA((30,)),
+            pltpu.SemaphoreType.DMA((30,)),
+        ],
+        compiler_params=pltpu.CompilerParams(collective_id=2, has_side_effects=True),
+    )(part, base)
+
+
+def dual_kernel(part, base, mapped, pulled_from, from_x, to_z, from_z, kept, send_sem, recv_sem):
+    z, x, y, z_peers, x_peer, y_peer = place()
+    rows, width = base.shape
+    half_rows = rows // 2
+    cols = lambda zz, xx: pl.ds(pl.multiple_of((zz * 2 + xx) * width, width), width)
+    greet(z_peers + [x_peer, y_peer])
+    sender = Sender(send_sem, recv_sem)
+    order = (2, 1, 3, 0)
+    first, third = {}, {}
+    for k in order:
+        first[k] = sender.send(part.at[:, cols(lax.rem(z + k, 4), 1 - x)], from_x.at[k], x_peer)
+    for k in order:
+        first[k].wait_recv()
+        total = part[:, cols(lax.rem(z + k, 4), x)].astype(F32) + from_x[k].astype(F32)
+        if k:
+            to_z[k - 1] = total.astype(BF16)
+            third[k] = sender.send(to_z.at[k - 1], from_z.at[k - 1], z_peers[k - 1])
+        else:
+            kept[...] = mapped[...] + total
+    for k in (1, 2, 3):
+        third[k].wait_recv()
+    grad = kept[...] + (from_z[0].astype(F32) + from_z[1].astype(F32) + from_z[2].astype(F32))
+    view = lambda zz, xx, yy: pulled_from.at[pl.ds(pl.multiple_of(yy * rows, rows), rows), cols(zz, xx)]
+    half = lambda zz, xx, yy, h: pulled_from.at[
+        pl.ds(pl.multiple_of(yy * rows + h * half_rows, half_rows), half_rows), cols(zz, xx)
+    ]
+    pulled_from[pl.ds(pl.multiple_of(y * rows, rows), rows), cols(z, x)] = (
+        base[...].astype(F32) - grad
+    ).astype(BF16)
+    gather_all(sender, view, half, z, x, y, z_peers, x_peer, y_peer, view(z, x, y))
+    sender.drain()
+
+
+def reduce_dual(part, base, mapped):
+    rows, width = base.shape
+    return pl.pallas_call(
+        dual_kernel,
+        out_shape=jax.ShapeDtypeStruct((2 * rows, part.shape[1]), BF16),
+        in_specs=[pl.BlockSpec(memory_space=pltpu.VMEM)] * 3,
+        out_specs=pl.BlockSpec(memory_space=pltpu.VMEM),
+        scratch_shapes=[
+            pltpu.VMEM((4, rows, width), BF16),
+            pltpu.VMEM((3, rows, width), BF16),
+            pltpu.VMEM((3, rows, width), BF16),
+            pltpu.VMEM((rows, width), F32),
+            pltpu.SemaphoreType.DMA((26,)),
+            pltpu.SemaphoreType.DMA((26,)),
+        ],
+        compiler_params=pltpu.CompilerParams(collective_id=3, has_side_effects=True),
+    )(part, base, mapped)
+
+
+def chip_body(
+    samples,
+    dual_weight,
+    dual_vector,
+    map_weight,
+    map_vector,
+    moment_weight,
+    square_weight,
+    moment_vector,
+    square_vector,
+):
+    swap = [(0, 1), (1, 0), (2, 3), (3, 2)]
+    fsdp, rep = lax.axis_index("fsdp"), lax.axis_index("rep")
+    weight = map_weight.astype(BF16)
+    vector = map_vector.astype(BF16)
+    weights = (weight, lax.ppermute(weight, "rep", swap))
+    vectors = (vector, lax.ppermute(vector, "rep", swap))
+    rows = gather_samples(samples)
+    inverse_rows = 1.0 / (rows.shape[0] * 2)
+    sigmas, scales = [], []
+    for block, pair in zip(weights, vectors):
+        sigma = jax.nn.sigmoid(contract_last(rows, block) + pair[1].astype(F32))
+        sigmas.append(sigma)
+        scales.append((pair[0].astype(F32) * sigma).astype(BF16))
+    part = (
+        jnp.dot(scales[0], weights[0], preferred_element_type=F32)
+        + jnp.dot(scales[1], weights[1], preferred_element_type=F32)
+    ).astype(BF16)
+    half, width = rows.shape[0] // 2, rows.shape[1] // 8
+    base = lax.dynamic_slice(rows, ((rep // 2) * half, fsdp * width), (half, width))
+    mapped, mapped_low = reduce_map(part, base)
+    dual_hidden = contract_last(mapped_low, dual_weight) + dual_vector[1]
+    dual_scaled = (dual_vector[0] * jax.nn.sigmoid(dual_hidden)).astype(BF16)
+    dual_part = jnp.dot(dual_scaled, dual_weight, preferred_element_type=F32).astype(BF16)
+    residual = reduce_dual(dual_part, base, mapped)
+    grads, smalls = [], []
+    for block, pair, sigma, scaled in zip(weights[::-1], vectors[::-1], sigmas[::-1], scales[::-1]):
+        readout = pair[0].astype(F32)
+        pulled = contract_last(residual, block)
+        curve = readout * (sigma * (1.0 - sigma)) * pulled
+        grads.append(contract_first(scaled, residual) + contract_first(curve.astype(BF16), rows))
+        smalls.append(jnp.stack([jnp.sum(sigma * pulled, axis=0), jnp.sum(curve, axis=0)]))
+    owner_weight = (grads[1] + lax.ppermute(grads[0], "rep", swap)) * inverse_rows
+    owner_vector = (smalls[1] + lax.ppermute(smalls[0], "rep", swap)) * inverse_rows
+    next_weight, next_moment_weight, next_square_weight = adam_update(
+        map_weight, owner_weight, moment_weight, square_weight
+    )
+    raw_vector, next_moment_vector, next_square_vector = adam_update(
+        map_vector, owner_vector, moment_vector, square_vector
+    )
+    next_vector = jnp.concatenate([jnp.maximum(raw_vector[0:1], 0.0), raw_vector[1:2]], axis=0)
+    return (
+        next_weight,
+        next_vector,
+        next_moment_weight,
+        next_square_weight,
+        next_moment_vector,
+        next_square_vector,
+    )
 
 
 def body(
@@ -98,8 +414,9 @@
 
 
 def solution(mesh):
+    by_chip = mesh.shape["fsdp"] == 8 and mesh.shape["rep"] == 4
     return jax.shard_map(
-        body,
+        chip_body if by_chip else body,
         mesh=mesh,
         in_specs=(
             P(("fsdp", "rep"), None),

time: 495 us -> 241 us (0.49)
  waiting for transfers between devices: 412 us -> 2.6 us
  Pallas kernels: 0 us -> 162 us
  other arithmetic: 19.1 us -> 5.01 us
  starting transfers between devices: 0.42 us -> 14.3 us
  between operations: 14.2 us -> 0.83 us
  matrix products: 39.4 us -> 49.1 us
  blocking collectives: 5.58 us -> 0 us
    psum x2 -> x0, waiting for transfers between devices: 176 us -> none  [the longest x1 88.6 us: body(): lax.psum(jnp.dot(dual_scaled, dual_weight, preferred_element_type=jnp.flo...]
    pallas_call x0 -> x3, Pallas kernels: none -> 162 us  [the longest x1 79.8 us: reduce_map(): pl.pallas_call(map_kernel, out_shape=(jax.ShapeDtypeStruct((rows, width),...]
    reduce_scatter x1 -> x0, waiting for transfers between devices: 125 us -> none  [body(): lax.psum_scatter(grad_slab, 'rep', scatter_dimension=0, tiled=True)]
    all_gather x2 -> x0, waiting for transfers between devices: 97.2 us -> none  [the longest x1 60.9 us: body(): lax.all_gather(map_weight.astype(jnp.bfloat16), 'rep', axis=0, tiled=True)]
    ppermute x0 -> x4, starting transfers between devices: none -> 14.3 us  [the longest x1 13.5 us: chip_body(): lax.ppermute(grads[0], 'rep', swap)]
    unnamed x7 -> x0, waiting for transfers between devices: 13.3 us -> none
    sub x2 -> x1, other arithmetic: 12 us -> 0.59 us  [adam_update(): return (param - update, moment_new, square_new)]
    dot_general x2 -> x3, matrix products: 15 us -> 21.6 us  [the longest x1 12 us: chip_body(): jnp.dot(dual_scaled, dual_weight, preferred_element_type=F32).astype(BF16)]
  transfers between devices with their start and end apart: 6 -> 4, of which waited for: 6 -> 1; matrix products, arithmetic and copies ran while one was open for 3% -> 7% of each run, Pallas kernels for 0% -> 14%
where the time goes in v1:
time: 241 us; the launch traced here: 238 us
  Pallas kernels  162 us (67%)
  matrix products  49.1 us (20%)
  starting transfers between devices  14.3 us (6%)
  other arithmetic  5.01 us (2%)
  local copies, waits for them, and re-layouts  4.09 us (2%)
  waiting for transfers between devices  2.6 us (1%)
    pallas_call x1, Pallas kernels, reduce_map(): pl.pallas_call(map_kernel, out_shape=(jax.ShapeDtypeStruct((rows, width),...  79.8 us
    pallas_call x1, Pallas kernels, reduce_dual(): pl.pallas_call(dual_kernel, out_shape=jax.ShapeDtypeStruct((2 * rows, par...  47.8 us
    pallas_call x1, Pallas kernels, gather_samples(): pl.pallas_call(gather_kernel, out_shape=jax.ShapeDtypeStruct((16, rows, w...  34.5 us
    dot_general x4, matrix products, contract_first(): lax.dot_general(left, right, (((0,), (0,)), ((), ())), preferred_element_...  15.6 us
    ppermute x1, starting transfers between devices, chip_body(): lax.ppermute(grads[0], 'rep', swap)  13.5 us
    dot_general x1, matrix products, chip_body(): jnp.dot(dual_scaled, dual_weight, preferred_element_type=F32).astype(BF16)  12 us
    dot_general x4, matrix products, contract_last(): lax.dot_general(left, right, (((1,), (1,)), ((), ())), preferred_element_...  11.9 us
    dot_general x1, matrix products, chip_body(): jnp.dot(scales[0], weights[0], preferred_element_type=F32)  5.37 us
  transfers between devices with their start and end apart: 4, of which 1 were waited for; matrix products, arithmetic and copies ran while one was open for 7% of the time, Pallas kernels for 14%

profile of v1, /device:TPU:17, one launch (start us, length us, event | category | flops | bytes accessed | tf_op | source)
XLA Modules:
  0.0 238.1 jit_solution(3109312045784021411)
XLA Ops:
  0.6 0.0 copy-start.9
  0.6 0.0 copy-start.8
  0.7 3.8 %convert_element_type.38 = bf16[256,4096]{1,0:T(8,128)(2,1)} convert(f32[256,4096]{1,0:T(8,128)} %param.12) | non-fusion elementwise | flops 1048576 | bytes 6291456 | tf_op jit(solution)/shard_map/convert_element_type | solution.py:302
  4.5 0.7 collective-permute-start.1
  5.1 0.0 copy-done.9
  5.1 0.1 collective-permute-start
  5.2 34.5 %shard_map.136 = bf16[16,24,4096]{2,1,0:T(8,128)(2,1)} custom-call(bf16[24,4096]{1,0:T(8,128)(2,1)} %own_ref.1), custom_call_target="tpu_custom_call" | custom-call | bytes 100000000 | tf_op jit(solution)/shard_map/pallas_call | solution.py:128
  39.8 0.0 copy-done.8
  39.8 0.6 fusion.34
  40.4 3.6 %fusion.14 = f32[384,256]{1,0:T(8,128)S(1)} fusion(bf16[384,4096]{1,0:T(8,128)(2,1)} %bitcast.28, bf16[256,4096]{1,0:T(8,128)(2,1)} %convert_element_type.38, f32[256]{0:T(256)S(1)} %bitcast.48), kind=kOutput, calls=%fused_computation.24 | convolution fusion | flops 805699584 | bytes 5637120 | tf_op jit(solution)/shard_map/dot_general | solution.py:16
  43.9 0.0 copy-start
  44.0 5.4 %fusion.29 = f32[384,4096]{1,0:T(8,128)} fusion(bf16[256,4096]{1,0:T(8,128)(2,1)} %convert_element_type.38, f32[384,256]{1,0:T(8,128)S(1)} %fusion.14, f32[256]{0:T(256)S(1)} %bitcast.33), kind=kOutput, calls=%fused_computation.43 | convolution fusion | flops 805502976 | bytes 8782848 | tf_op jit(solution)/shard_map/dot_general | solution.py:314
  49.3 0.0 copy-done
  49.3 0.0 copy-start.2
  49.3 0.7 dynamic_slice.3.base
  50.0 0.0 collective-permute-done
  50.0 0.0 collective-permute-done.1
  50.0 3.0 %fusion.10 = f32[384,256]{1,0:T(8,128)S(1)} fusion(bf16[384,4096]{1,0:T(8,128)(2,1)S(1)} %bitcast.30, bf16[256,4096]{1,0:T(8,128)(2,1)} %collective-permute-done.1, f32[256]{0:T(256)S(1)} %bitcast.47), kind=kOutput, calls=%fused_computation.19 | convolution fusion | flops 805699584 | bytes 5637120 | tf_op jit(solution)/shard_map/dot_general | solution.py:16
  53.0 0.0 copy-start.6
  53.0 0.7 copy-done.6
  53.8 0.0 copy-done.2
  53.8 0.0 copy-start.10
  53.8 4.2 %add_convert_fusion.part = bf16[384,4096]{1,0:T(8,128)(2,1)} fusion(f32[384,4096]{1,0:T(8,128)S(1)} %copy-done.2, bf16[256,4096]{1,0:T(8,128)(2,1)} %collective-permute-done.1, f32[384,256]{1,0:T(8,128)S(1)} %fusion.10, f32[256]{0:T(256)S(1)} %bitcast.37), kind=kOutput, calls=%fused_computation | convolution fusion | flops 808648704 | bytes 11928576 | tf_op jit(solution)/shard_map/dot_general | solution.py:315
  58.0 79.8 %shard_map.137 = (f32[192,512]{1,0:T(8,128)}, bf16[192,4096]{1,0:T(8,128)(2,1)}) custom-call(bf16[384,4096]{1,0:T(8,128)(2,1)} %add_convert_fusion.part, bf16[192,512]{1,0:T(8,128)(2,1)} %dynamic_slice.3.base), custom_call_target="tpu_custom_call" | custom-call | tf_op jit(solution)/shard_map/pallas_call | solution.py:213
  137.8 0.0 copy-done.10
  137.8 12.0 %convolution_convert_fusion.part = bf16[192,4096]{1,0:T(8,128)(2,1)} fusion(bf16[1024,4096]{1,0:T(8,128)(2,1)} %param.10, bf16[192,4096]{1,0:T(8,128)(2,1)} %get-tuple-element.8, f32[1024]{0:T(1024)} %bitcast.42, f32[1024]{0:T(1024)S(1)} %bitcast.41), kind=kOutput, calls=%fused_computation.4 | convolution fusion | flops 3223191552 | bytes 11542528 | tf_op jit(solution)/shard_map/dot_general | solution.py:322
  149.8 47.8 %shard_map.138 = bf16[384,4096]{1,0:T(8,128)(2,1)} custom-call(bf16[192,4096]{1,0:T(8,128)(2,1)} %convolution_convert_fusion.part, bf16[192,512]{1,0:T(8,128)(2,1)} %dynamic_slice.3.base, f32[192,512]{1,0:T(8,128)} %get-tuple-element.9.mapped), custom_call_target="tpu_custom_call" | custom-call | tf_op jit(solution)/shard_map/pallas_call | solution.py:272
  197.6 0.0 copy-start.1
  197.7 0.0 copy-start.7
  197.7 3.4 %fusion.30 = f32[256,4096]{1,0:T(8,128)S(1)} fusion(bf16[384,4096]{1,0:T(8,128)(2,1)} %shard_map.138, f32[384,256]{1,0:T(8,128)} %copy-done.6, f32[256]{0:T(256)S(1)} %bitcast.38), kind=kOutput, calls=%fused_computation.44 | convolution fusion | flops 805502976 | bytes 7734272 | tf_op jit(solution)/shard_map/dot_general | solution.py:22
  201.1 0.0 copy-done.1
  201.1 0.0 copy-done.7
  201.1 2.6 %multiply_reduce_fusion = (f32[256]{0:T(256)S(1)}, f32[256]{0:T(256)S(1)}, f32[384,256]{1,0:T(8,128)S(1)}) fusion(f32[384,256]{1,0:T(8,128)S(1)} %copy-done.7, f32[256]{0:T(256)S(1)} %bitcast.39, bf16[384,4096]{1,0:T(8,128)(2,1)S(1)} %copy-done.1, bf16[256,4096]{1,0:T(8,128)(2,1)} %collective-permute-done.1), kind=kOutput, calls=%fused_computation.31 | convolution fusion | flops 805993984 | bytes 6032384 | tf_op jit(solution)/shard_map/dot_general | solution.py:16
  203.8 1.5 convolution_add_fusion
  205.3 13.5 %collective-permute-start.2 = (f32[256,4096]{1,0:T(8,128)S(1)}, f32[256,4096]{1,0:T(8,128)S(1)}, u32[]{:S(2)}, u32[]{:S(2)}) collective-permute-start(f32[256,4096]{1,0:T(8,128)S(1)} %convolution_add_fusion), channel_id=1, source_target_pairs={{0,1},{1,0},{2,3},{3,2},{4,5},{5,4},{6,7},{7,6},{8,9},{9,8},{10,11... | collective-permute-start | bytes 12582920 | tf_op jit(solution)/shard_map/ppermute | solution.py:331
  218.8 0.1 collective-permute-start.3
  218.9 0.0 copy-start.4
  218.9 2.8 %multiply_reduce_fusion.1 = (f32[256]{0:T(256)S(1)}, f32[256]{0:T(256)S(1)}, f32[384,256]{1,0:T(8,128)S(1)}) fusion(f32[384,256]{1,0:T(8,128)S(1)} %fusion.14, f32[256]{0:T(256)S(1)} %bitcast.34, bf16[384,4096]{1,0:T(8,128)(2,1)S(1)} %copy-done.1, bf16[256,4096]{1,0:T(8,128)(2,1)} %convert_element_type.38), kind=kOutput, calls=%fused_computation.32 | convolution fusion | flops 805993984 | bytes 6032384 | tf_op jit(solution)/shard_map/dot_general | solution.py:16
  221.7 0.0 copy-start.11
  221.7 0.0 copy-start.12
  221.7 0.0 copy-start.3
  221.7 1.3 fusion.28
  223.0 2.6 %collective-permute-done.3 = f32[2,256]{1,0:T(2,128)S(1)} collective-permute-done((f32[2,256]{1,0:T(2,128)S(1)}, f32[2,256]{1,0:T(2,128)S(1)}, u32[]{:S(2)}, u32[]{:S(2)}) %collective-permute-start.3) | collective-permute-done | bytes 2080 | tf_op jit(solution)/shard_map/ppermute | solution.py:332
  225.6 0.0 copy-done.11
  225.6 0.0 copy-done.12
  225.6 0.6 divide_subtract_fusion.1
  226.2 0.6 pad_maximum_fusion.1
  226.8 0.0 collective-permute-done.2
  226.8 0.0 copy-start.5
  226.8 2.0 copy-done.5
  228.8 0.0 copy-done.4
  228.8 0.0 copy-done.3
  228.8 9.3 %divide_subtract_fusion = (f32[256,4096]{1,0:T(8,128)}, f32[256,4096]{1,0:T(8,128)}, f32[256,4096]{1,0:T(8,128)}) fusion(f32[256,4096]{1,0:T(8,128)S(1)} %copy-done.3, f32[256,4096]{1,0:T(8,128)S(1)} %copy-done.4, f32[256,4096]{1,0:T(8,128)} %param.15, f32[256,4096]{1,0:T(8,128)} %copy-done.5, f32[256,4096]{1,0:T(8,128)S(1)} %fusion.28, ...), kind=kOutput, calls=%fused_computation.5 | convolution fusion | flops 821526528 | bytes 37487616 | tf_op jit(solution)/shard_map/dot_general | solution.py:22
  (5 shorter events, 0.0 us)
Async XLA Ops:
  0.6 4.5 %copy-start.9 = (f32[2,256]{1,0:T(2,128)S(1)}, f32[2,256]{1,0:T(2,128)}, u32[]{:S(2)}) copy-start(f32[2,256]{1,0:T(2,128)} %param.13) | copy-start | bytes 6148
  0.6 39.1 %copy-start.8 = (f32[2,1024]{1,0:T(2,128)S(1)}, f32[2,1024]{1,0:T(2,128)}, u32[]{:S(2)}) copy-start(f32[2,1024]{1,0:T(2,128)} %param.11) | copy-start | bytes 24580
  4.5 45.6 %collective-permute-start.1 = (bf16[256,4096]{1,0:T(8,128)(2,1)}, bf16[256,4096]{1,0:T(8,128)(2,1)}, u32[]{:S(2)}, u32[]{:S(2)}) collective-permute-start(bf16[256,4096]{1,0:T(8,128)(2,1)} %convert_element_type.38), channel_id=1, source_target_pairs={{0,1},{1,0},{2,3},{3,2},{4,5},{5,4},{6,7},{7,6},{8,9},{9,8},{10,11... | collective-permute-start | bytes 6291464 | tf_op jit(solution)/shard_map/ppermute | solution.py:304
  5.1 44.9 %collective-permute-start = (bf16[2,256]{1,0:T(2,128)(2,1)S(1)}, bf16[2,256]{1,0:T(2,128)(2,1)S(1)}, u32[]{:S(2)}, u32[]{:S(2)}) collective-permute-start(bf16[2,256]{1,0:T(2,128)(2,1)S(1)} %convert_element_type.37), channel_id=1, source_target_pairs={{0,1},{1,0},{2,3},{3,2},{4,5},{5,4},{6,7},{7,6},{8,9},{9,8},{10,11... | collective-permute-start | bytes 3080 | tf_op jit(solution)/shard_map/ppermute | solution.py:305
  43.9 5.4 %copy-start = (bf16[16,24,4096]{2,1,0:T(8,128)(2,1)S(1)}, bf16[16,24,4096]{2,1,0:T(8,128)(2,1)}, u32[]{:S(2)}) copy-start(bf16[16,24,4096]{2,1,0:T(8,128)(2,1)} %shard_map.136) | copy-start | bytes 9437188
  49.3 4.5 %copy-start.2 = (f32[384,4096]{1,0:T(8,128)S(1)}, f32[384,4096]{1,0:T(8,128)}, u32[]{:S(2)}) copy-start(f32[384,4096]{1,0:T(8,128)} %fusion.29) | copy-start | bytes 18874372
  53.0 0.7 copy-start.6
  53.8 84.0 %copy-start.10 = (f32[1,1024]{1,0:T(1,128)S(1)}, f32[1,1024]{1,0:T(1,128)}, u32[]{:S(2)}) copy-start(f32[1,1024]{1,0:T(1,128)} %get-tuple-element.20) | copy-start | bytes 12292
  197.6 3.5 %copy-start.1 = (bf16[384,4096]{1,0:T(8,128)(2,1)S(1)}, bf16[384,4096]{1,0:T(8,128)(2,1)}, u32[]{:S(2)}) copy-start(bf16[384,4096]{1,0:T(8,128)(2,1)} %shard_map.138) | copy-start | bytes 9437188
  197.7 3.5 %copy-start.7 = (f32[384,256]{1,0:T(8,128)S(1)}, f32[384,256]{1,0:T(8,128)}, u32[]{:S(2)}) copy-start(f32[384,256]{1,0:T(8,128)} %copy-done.6) | copy-start | bytes 1179652
  205.3 21.5 %collective-permute-start.2 = (f32[256,4096]{1,0:T(8,128)S(1)}, f32[256,4096]{1,0:T(8,128)S(1)}, u32[]{:S(2)}, u32[]{:S(2)}) collective-permute-start(f32[256,4096]{1,0:T(8,128)S(1)} %convolution_add_fusion), channel_id=1, source_target_pairs={{0,1},{1,0},{2,3},{3,2},{4,5},{5,4},{6,7},{7,6},{8,9},{9,8},{10,11... | collective-permute-start | bytes 12582920 | tf_op jit(solution)/shard_map/ppermute | solution.py:331
  218.8 6.8 %collective-permute-start.3 = (f32[2,256]{1,0:T(2,128)S(1)}, f32[2,256]{1,0:T(2,128)S(1)}, u32[]{:S(2)}, u32[]{:S(2)}) collective-permute-start(f32[2,256]{1,0:T(2,128)S(1)} %pad_maximum_fusion), channel_id=1, source_target_pairs={{0,1},{1,0},{2,3},{3,2},{4,5},{5,4},{6,7},{7,6},{8,9},{9,8},{10,11... | collective-permute-start | bytes 6152 | tf_op jit(solution)/shard_map/ppermute | solution.py:332
  218.9 9.9 %copy-start.4 = (f32[256,4096]{1,0:T(8,128)S(1)}, f32[256,4096]{1,0:T(8,128)}, u32[]{:S(2)}) copy-start(f32[256,4096]{1,0:T(8,128)} %param.14) | copy-start | bytes 12582916
  221.7 3.9 %copy-start.11 = (f32[2,256]{1,0:T(2,128)S(1)}, f32[2,256]{1,0:T(2,128)}, u32[]{:S(2)}) copy-start(f32[2,256]{1,0:T(2,128)} %param.16) | copy-start | bytes 6148
  221.7 3.9 %copy-start.12 = (f32[2,256]{1,0:T(2,128)S(1)}, f32[2,256]{1,0:T(2,128)}, u32[]{:S(2)}) copy-start(f32[2,256]{1,0:T(2,128)} %param.17) | copy-start | bytes 6148
  221.7 7.1 %copy-start.3 = (f32[256,4096]{1,0:T(8,128)S(1)}, f32[256,4096]{1,0:T(8,128)}, u32[]{:S(2)}) copy-start(f32[256,4096]{1,0:T(8,128)} %param.12) | copy-start | bytes 12582916
  226.8 2.0 copy-start.5

commit v2 on v1

--- a/solution.py
+++ b/solution.py
@@ -141,75 +141,109 @@
     return gathered.reshape(16 * rows, width)
 
 
-def map_kernel(
-    part, base, mapped, low, from_y, from_x, to_x, to_y, late_x, late_y, to_z, from_z, send_sem, recv_sem
+ORDER = (2, 1, 3, 0)
+ARRIVAL = (0, 1, 3, 2)
+CHUNKS = 2
+
+
+def interleave(first, second, schedule):
+    for which in schedule:
+        next((first, second)[which])
+
+
+def map_steps(
+    chunk, sender, spot, cut, part, base, mapped, low, from_y, from_x, to_x, to_y, late_x, late_y, to_z, from_z
 ):
-    z, x, y, z_peers, x_peer, y_peer = place()
+    z, x, y, z_peers, x_peer, y_peer = spot
     rows, width = base.shape
-    half = rows // 2
+    span = rows // CHUNKS
     cols = lambda zz, xx: pl.ds(pl.multiple_of((zz * 2 + xx) * width, width), width)
-    lines = lambda yy, h: pl.ds(pl.multiple_of(yy * rows + h * half, half), half)
+    top_rows = lambda yy: pl.ds(pl.multiple_of(yy * rows + chunk * span, 16), cut)
+    low_rows = lambda yy: pl.ds(pl.multiple_of(yy * rows + chunk * span + cut, 16), span - cut)
     lane = lambda xx: pl.ds(pl.multiple_of(xx * width, width), width)
-    greet(z_peers + [x_peer, y_peer])
-    sender = Sender(send_sem, recv_sem)
-    order = (2, 1, 3, 0)
-    first_y, first_x = {}, {}
-    for k in order:
+    here = slice(chunk * span, (chunk + 1) * span)
+    from_y, from_x, to_x, to_y, late_x, late_y, to_z, from_z = (
+        ref.at[chunk] for ref in (from_y, from_x, to_x, to_y, late_x, late_y, to_z, from_z)
+    )
+    first_y, first_x, second_x, second_y, third = {}, {}, {}, {}, {}
+    for k in ORDER:
         zz = lax.rem(z + k, 4)
         pair = pl.ds(pl.multiple_of(zz * 2 * width, 2 * width), 2 * width)
-        first_y[k] = sender.send(part.at[lines(1 - y, 0), pair], from_y.at[k], y_peer)
+        first_y[k] = sender.send(part.at[top_rows(1 - y), pair], from_y.at[k], y_peer)
         first_x[k] = [
-            sender.send(part.at[lines(yy, 1), cols(zz, 1 - x)], from_x.at[k, yy], x_peer) for yy in (0, 1)
+            sender.send(part.at[low_rows(yy), cols(zz, 1 - x)], from_x.at[k, yy], x_peer) for yy in (0, 1)
         ]
-    second_x, second_y = {}, {}
-    for k in order:
+        yield
+    for k in ORDER:
         zz = lax.rem(z + k, 4)
         first_y[k].wait_recv()
         to_x[k] = (
-            part[lines(y, 0), cols(zz, 1 - x)].astype(F32) + from_y[k, :, lane(1 - x)].astype(F32)
+            part[top_rows(y), cols(zz, 1 - x)].astype(F32) + from_y[k, :, lane(1 - x)].astype(F32)
         ).astype(BF16)
         second_x[k] = sender.send(to_x.at[k], late_x.at[k], x_peer)
         for copy in first_x[k]:
             copy.wait_recv()
         to_y[k] = (
-            part[lines(1 - y, 1), cols(zz, x)].astype(F32) + from_x[k, 1 - y].astype(F32)
+            part[low_rows(1 - y), cols(zz, x)].astype(F32) + from_x[k, 1 - y].astype(F32)
         ).astype(BF16)
         second_y[k] = sender.send(to_y.at[k], late_y.at[k], y_peer)
-    third = {}
-    for k in order:
+        yield
+    for k in ORDER:
         zz = lax.rem(z + k, 4)
         second_x[k].wait_recv()
         top = (
-            part[lines(y, 0), cols(zz, x)].astype(F32)
+            part[top_rows(y), cols(zz, x)].astype(F32)
             + from_y[k, :, lane(x)].astype(F32)
             + late_x[k].astype(F32)
         )
         second_y[k].wait_recv()
         bottom = (
-            part[lines(y, 1), cols(zz, x)].astype(F32) + from_x[k, y].astype(F32) + late_y[k].astype(F32)
+            part[low_rows(y), cols(zz, x)].astype(F32) + from_x[k, y].astype(F32) + late_y[k].astype(F32)
         )
         if k:
-            to_z[k - 1, :half] = top.astype(BF16)
-            to_z[k - 1, half:] = bottom.astype(BF16)
+            to_z[k - 1, :cut] = top.astype(BF16)
+            to_z[k - 1, cut:] = bottom.astype(BF16)
             third[k] = sender.send(to_z.at[k - 1], from_z.at[k - 1], z_peers[k - 1])
         else:
-            mapped[:half] = top + base[:half].astype(F32)
-            mapped[half:] = bottom + base[half:].astype(F32)
+            total = jnp.concatenate([top, bottom], axis=0) + base[here].astype(F32)
+        yield
     for k in (1, 2, 3):
         third[k].wait_recv()
-    total = mapped[...] + (from_z[0].astype(F32) + from_z[1].astype(F32) + from_z[2].astype(F32))
-    mapped[...] = total
-    low[:, cols(z, x)] = total.astype(BF16)
-    view = lambda zz, xx, yy: low.at[:, cols(zz, xx)]
-    over_x, _ = gather_line(sender, view, z, x, y, z_peers, x_peer, None, view(z, x, y))
+    total = total + (from_z[0].astype(F32) + from_z[1].astype(F32) + from_z[2].astype(F32))
+    mapped[here] = total
+    low[here, cols(z, x)] = total.astype(BF16)
+    own = low.at[here, cols(z, x)]
+    to_line = [sender.send(own, own, peer) for peer in z_peers]
+    over_x = [sender.send(own, own, x_peer)]
+    yield
+    for k in (1, 3, 2):
+        to_line[k - 1].wait_recv()
+        block = low.at[here, cols(lax.rem(z + 4 - k, 4), x)]
+        over_x.append(sender.send(block, block, x_peer))
+        yield
     for copy in over_x:
         copy.wait_recv()
+    yield
+
+
+MAP_SCHEDULE = [0] * 4 + [0, 1] * 8 + [0, 1, 1, 0, 1, 0, 1, 0, 1, 1, 1, 1, 1, 0]
+
+
+def map_kernel(part, base, mapped, low, *rest):
+    scratch, (send_sem, recv_sem) = rest[:-2], rest[-2:]
+    spot = place()
+    greet(spot[3] + list(spot[4:]))
+    sender = Sender(send_sem, recv_sem)
+    cut = scratch[2].shape[2]
+    steps = [map_steps(c, sender, spot, cut, part, base, mapped, low, *scratch) for c in range(CHUNKS)]
+    interleave(steps[0], steps[1], MAP_SCHEDULE)
     sender.drain()
 
 
 def reduce_map(part, base):
     rows, width = base.shape
-    half = rows // 2
+    span = rows // CHUNKS
+    cut = span // 3 * 2
     return pl.pallas_call(
         map_kernel,
         out_shape=(
@@ -219,68 +253,108 @@
         in_specs=[pl.BlockSpec(memory_space=pltpu.VMEM)] * 2,
         out_specs=[pl.BlockSpec(memory_space=pltpu.VMEM)] * 2,
         scratch_shapes=[
-            pltpu.VMEM((4, half, 2 * width), BF16),
-            pltpu.VMEM((4, 2, half, width), BF16),
-            pltpu.VMEM((4, half, width), BF16),
-            pltpu.VMEM((4, half, width), BF16),
-            pltpu.VMEM((4, half, width), BF16),
-            pltpu.VMEM((4, half, width), BF16),
-            pltpu.VMEM((3, rows, width), BF16),
-            pltpu.VMEM((3, rows, width), BF16),
-            pltpu.SemaphoreType.DMA((30,)),
-            pltpu.SemaphoreType.DMA((30,)),
+            pltpu.VMEM((CHUNKS, 4, cut, 2 * width), BF16),
+            pltpu.VMEM((CHUNKS, 4, 2, span - cut, width), BF16),
+            pltpu.VMEM((CHUNKS, 4, cut, width), BF16),
+            pltpu.VMEM((CHUNKS, 4, span - cut, width), BF16),
+            pltpu.VMEM((CHUNKS, 4, cut, width), BF16),
+            pltpu.VMEM((CHUNKS, 4, span - cut, width), BF16),
+            pltpu.VMEM((CHUNKS, 3, span, width), BF16),
+            pltpu.VMEM((CHUNKS, 3, span, width), BF16),
+            pltpu.SemaphoreType.DMA((30 * CHUNKS,)),
+            pltpu.SemaphoreType.DMA((30 * CHUNKS,)),
         ],
         compiler_params=pltpu.CompilerParams(collective_id=2, has_side_effects=True),
     )(part, base)
 
 
-def dual_kernel(part, base, mapped, pulled_from, from_x, to_z, from_z, kept, send_sem, recv_sem):
-    z, x, y, z_peers, x_peer, y_peer = place()
+def dual_steps(chunk, sender, spot, part, base, mapped, full, from_x, to_z, from_z):
+    z, x, y, z_peers, x_peer, y_peer = spot
     rows, width = base.shape
-    half_rows = rows // 2
+    span = rows // CHUNKS
+    cut = span // 3 * 2
     cols = lambda zz, xx: pl.ds(pl.multiple_of((zz * 2 + xx) * width, width), width)
-    greet(z_peers + [x_peer, y_peer])
-    sender = Sender(send_sem, recv_sem)
-    order = (2, 1, 3, 0)
+    here = slice(chunk * span, (chunk + 1) * span)
+    view = lambda zz, xx, yy: full.at[
+        pl.ds(pl.multiple_of(yy * rows + chunk * span, 16), span), cols(zz, xx)
+    ]
+    top = lambda zz, xx, yy: full.at[pl.ds(pl.multiple_of(yy * rows + chunk * span, 16), cut), cols(zz, xx)]
+    bottom = lambda zz, xx, yy: full.at[
+        pl.ds(pl.multiple_of(yy * rows + chunk * span + cut, 16), span - cut), cols(zz, xx)
+    ]
+    from_x, to_z, from_z = (ref.at[chunk] for ref in (from_x, to_z, from_z))
     first, third = {}, {}
-    for k in order:
-        first[k] = sender.send(part.at[:, cols(lax.rem(z + k, 4), 1 - x)], from_x.at[k], x_peer)
-    for k in order:
+    for k in ORDER:
+        first[k] = sender.send(part.at[here, cols(lax.rem(z + k, 4), 1 - x)], from_x.at[k], x_peer)
+        yield
+    for k in ORDER:
         first[k].wait_recv()
-        total = part[:, cols(lax.rem(z + k, 4), x)].astype(F32) + from_x[k].astype(F32)
+        total = part[here, cols(lax.rem(z + k, 4), x)].astype(F32) + from_x[k].astype(F32)
         if k:
             to_z[k - 1] = total.astype(BF16)
             third[k] = sender.send(to_z.at[k - 1], from_z.at[k - 1], z_peers[k - 1])
-        else:
-            kept[...] = mapped[...] + total
+        yield
     for k in (1, 2, 3):
         third[k].wait_recv()
-    grad = kept[...] + (from_z[0].astype(F32) + from_z[1].astype(F32) + from_z[2].astype(F32))
-    view = lambda zz, xx, yy: pulled_from.at[pl.ds(pl.multiple_of(yy * rows, rows), rows), cols(zz, xx)]
-    half = lambda zz, xx, yy, h: pulled_from.at[
-        pl.ds(pl.multiple_of(yy * rows + h * half_rows, half_rows), half_rows), cols(zz, xx)
+    grad = (mapped[here] + total) + (
+        from_z[0].astype(F32) + from_z[1].astype(F32) + from_z[2].astype(F32)
+    )
+    full[pl.ds(pl.multiple_of(y * rows + chunk * span, 16), span), cols(z, x)] = (
+        base[here].astype(F32) - grad
+    ).astype(BF16)
+    own = view(z, x, y)
+    to_line = [sender.send(own, own, peer) for peer in z_peers]
+    over_x, over_y = [sender.send(own, own, x_peer)], [sender.send(own, own, y_peer)]
+    yield
+    for k in ARRIVAL[1:]:
+        to_line[k - 1].wait_recv()
+        block = view(lax.rem(z + 4 - k, 4), x, y)
+        over_x.append(sender.send(block, block, x_peer))
+        over_y.append(sender.send(block, block, y_peer))
+        yield
+    diagonal = []
+    for i, k in enumerate(ARRIVAL):
+        source = lax.rem(z + 4 - k, 4)
+        over_x[i].wait_recv()
+        block = top(source, 1 - x, y)
+        diagonal.append(sender.send(block, block, y_peer))
+        over_y[i].wait_recv()
+        block = bottom(source, x, 1 - y)
+        diagonal.append(sender.send(block, block, x_peer))
+        yield
+    for copy in diagonal:
+        copy.wait_recv()
+    yield
+
+
+DUAL_SCHEDULE = [0] * 4 + [0, 1] * 4 + [0, 1, 0, 1, 0, 1, 0, 1, 1] + [0, 1] * 3 + [0] + [1] * 4 + [0, 1]
+
+
+def dual_kernel(part, base, mapped, full, from_x, to_z, from_z, send_sem, recv_sem):
+    spot = place()
+    greet(spot[3] + list(spot[4:]))
+    sender = Sender(send_sem, recv_sem)
+    steps = [
+        dual_steps(c, sender, spot, part, base, mapped, full, from_x, to_z, from_z) for c in range(CHUNKS)
     ]
-    pulled_from[pl.ds(pl.multiple_of(y * rows, rows), rows), cols(z, x)] = (
-        base[...].astype(F32) - grad
-    ).astype(BF16)
-    gather_all(sender, view, half, z, x, y, z_peers, x_peer, y_peer, view(z, x, y))
+    interleave(steps[0], steps[1], DUAL_SCHEDULE)
     sender.drain()
 
 
 def reduce_dual(part, base, mapped):
     rows, width = base.shape
+    span = rows // CHUNKS
     return pl.pallas_call(
         dual_kernel,
         out_shape=jax.ShapeDtypeStruct((2 * rows, part.shape[1]), BF16),
         in_specs=[pl.BlockSpec(memory_space=pltpu.VMEM)] * 3,
         out_specs=pl.BlockSpec(memory_space=pltpu.VMEM),
         scratch_shapes=[
-            pltpu.VMEM((4, rows, width), BF16),
-            pltpu.VMEM((3, rows, width), BF16),
-            pltpu.VMEM((3, rows, width), BF16),
-            pltpu.VMEM((rows, width), F32),
-            pltpu.SemaphoreType.DMA((26,)),
-            pltpu.SemaphoreType.DMA((26,)),
+            pltpu.VMEM((CHUNKS, 4, span, width), BF16),
+            pltpu.VMEM((CHUNKS, 3, span, width), BF16),
+            pltpu.VMEM((CHUNKS, 3, span, width), BF16),
+            pltpu.SemaphoreType.DMA((26 * CHUNKS,)),
+            pltpu.SemaphoreType.DMA((26 * CHUNKS,)),
         ],
         compiler_params=pltpu.CompilerParams(collective_id=3, has_side_effects=True),
     )(part, base, mapped)

time: 241 us -> 225 us (0.934); the launches traced: 238 us -> 225 us
  starting transfers between devices: 14.3 us -> 4.59 us
  Pallas kernels: 162 us -> 158 us
    pallas_call x1, Pallas kernels: 79.8 us -> 69.1 us  [reduce_map(): pl.pallas_call(map_kernel, out_shape=(jax.ShapeDtypeStruct((rows, width),...]
    ppermute x1, starting transfers between devices: 13.5 us -> 3.76 us  [chip_body(): lax.ppermute(grads[0], 'rep', swap)]
    pallas_call x1, Pallas kernels: 47.8 us -> 54.7 us  [reduce_dual(): pl.pallas_call(dual_kernel, out_shape=jax.ShapeDtypeStruct((2 * rows, par...]
  transfers between devices with their start and end apart: 4 -> 4, of which waited for: 1 -> 1; matrix products, arithmetic and copies ran while one was open for 7% -> 7% of each run, Pallas kernels for 14% -> 15%
where the time goes in v2:
time: 225 us
  Pallas kernels  158 us (70%)
  matrix products  49.1 us (22%)
  other arithmetic  5.01 us (2%)
  starting transfers between devices  4.59 us (2%)
  local copies, waits for them, and re-layouts  4.09 us (2%)
  waiting for transfers between devices  2.61 us (1%)
    pallas_call x1, Pallas kernels, reduce_map(): pl.pallas_call(map_kernel, out_shape=(jax.ShapeDtypeStruct((rows, width),...  69.1 us
    pallas_call x1, Pallas kernels, reduce_dual(): pl.pallas_call(dual_kernel, out_shape=jax.ShapeDtypeStruct((2 * rows, par...  54.7 us
    pallas_call x1, Pallas kernels, gather_samples(): pl.pallas_call(gather_kernel, out_shape=jax.ShapeDtypeStruct((16, rows, w...  34.5 us
    dot_general x4, matrix products, contract_first(): lax.dot_general(left, right, (((0,), (0,)), ((), ())), preferred_element_...  15.4 us
    dot_general x4, matrix products, contract_last(): lax.dot_general(left, right, (((1,), (1,)), ((), ())), preferred_element_...  12.1 us
    dot_general x1, matrix products, chip_body(): jnp.dot(dual_scaled, dual_weight, preferred_element_type=F32).astype(BF16)  12 us
    dot_general x1, matrix products, chip_body(): jnp.dot(scales[0], weights[0], preferred_element_type=F32)  5.37 us
  transfers between devices with their start and end apart: 4, of which 1 were waited for; matrix products, arithmetic and copies ran while one was open for 7% of the time, Pallas kernels for 15%

profile of v2, /device:TPU:17, one launch (start us, length us, event | category | flops | bytes accessed | tf_op | source)
XLA Modules:
  0.0 224.6 jit_solution(13298546053444239170)
XLA Ops:
  0.6 0.0 copy-start.9
  0.6 0.0 copy-start.8
  0.7 3.8 %convert_element_type.38 = bf16[256,4096]{1,0:T(8,128)(2,1)} convert(f32[256,4096]{1,0:T(8,128)} %param.12) | non-fusion elementwise | flops 1048576 | bytes 6291456 | tf_op jit(solution)/shard_map/convert_element_type | solution.py:376
  4.5 0.7 collective-permute-start.1
  5.1 0.0 copy-done.9
  5.1 0.1 collective-permute-start
  5.2 34.5 %shard_map.136 = bf16[16,24,4096]{2,1,0:T(8,128)(2,1)} custom-call(bf16[24,4096]{1,0:T(8,128)(2,1)} %own_ref.1), custom_call_target="tpu_custom_call" | custom-call | bytes 100000000 | tf_op jit(solution)/shard_map/pallas_call | solution.py:128
  39.8 0.0 copy-done.8
  39.8 0.6 fusion.34
  40.4 3.6 %fusion.14 = f32[384,256]{1,0:T(8,128)S(1)} fusion(bf16[384,4096]{1,0:T(8,128)(2,1)} %bitcast.28, bf16[256,4096]{1,0:T(8,128)(2,1)} %convert_element_type.38, f32[256]{0:T(256)S(1)} %bitcast.48), kind=kOutput, calls=%fused_computation.24 | convolution fusion | flops 805699584 | bytes 5637120 | tf_op jit(solution)/shard_map/dot_general | solution.py:16
  43.9 0.0 copy-start
  44.0 5.4 %fusion.29 = f32[384,4096]{1,0:T(8,128)} fusion(bf16[256,4096]{1,0:T(8,128)(2,1)} %convert_element_type.38, f32[384,256]{1,0:T(8,128)S(1)} %fusion.14, f32[256]{0:T(256)S(1)} %bitcast.33), kind=kOutput, calls=%fused_computation.43 | convolution fusion | flops 805502976 | bytes 8782848 | tf_op jit(solution)/shard_map/dot_general | solution.py:388
  49.3 0.0 copy-done
  49.3 0.0 copy-start.2
  49.3 0.7 dynamic_slice.3.base
  50.0 0.0 collective-permute-done
  50.0 0.0 collective-permute-done.1
  50.0 3.0 %fusion.10 = f32[384,256]{1,0:T(8,128)S(1)} fusion(bf16[384,4096]{1,0:T(8,128)(2,1)S(1)} %bitcast.30, bf16[256,4096]{1,0:T(8,128)(2,1)} %collective-permute-done.1, f32[256]{0:T(256)S(1)} %bitcast.47), kind=kOutput, calls=%fused_computation.19 | convolution fusion | flops 805699584 | bytes 5637120 | tf_op jit(solution)/shard_map/dot_general | solution.py:16
  53.0 0.0 copy-start.6
  53.0 0.7 copy-done.6
  53.8 0.0 copy-done.2
  53.8 0.0 copy-start.10
  53.8 4.2 %add_convert_fusion.part = bf16[384,4096]{1,0:T(8,128)(2,1)} fusion(f32[384,4096]{1,0:T(8,128)S(1)} %copy-done.2, bf16[256,4096]{1,0:T(8,128)(2,1)} %collective-permute-done.1, f32[384,256]{1,0:T(8,128)S(1)} %fusion.10, f32[256]{0:T(256)S(1)} %bitcast.37), kind=kOutput, calls=%fused_computation | convolution fusion | flops 808648704 | bytes 11928576 | tf_op jit(solution)/shard_map/dot_general | solution.py:389
  58.0 69.1 %shard_map.137 = (f32[192,512]{1,0:T(8,128)}, bf16[192,4096]{1,0:T(8,128)(2,1)}) custom-call(bf16[384,4096]{1,0:T(8,128)(2,1)} %add_convert_fusion.part, bf16[192,512]{1,0:T(8,128)(2,1)} %dynamic_slice.3.base), custom_call_target="tpu_custom_call" | custom-call | tf_op jit(solution)/shard_map/pallas_call | solution.py:247
  127.1 0.0 copy-done.10
  127.1 12.0 %convolution_convert_fusion.part = bf16[192,4096]{1,0:T(8,128)(2,1)} fusion(bf16[1024,4096]{1,0:T(8,128)(2,1)} %param.10, bf16[192,4096]{1,0:T(8,128)(2,1)} %get-tuple-element.8, f32[1024]{0:T(1024)} %bitcast.42, f32[1024]{0:T(1024)S(1)} %bitcast.41), kind=kOutput, calls=%fused_computation.4 | convolution fusion | flops 3223191552 | bytes 11542528 | tf_op jit(solution)/shard_map/dot_general | solution.py:396
  139.1 54.7 %shard_map.138 = bf16[384,4096]{1,0:T(8,128)(2,1)} custom-call(bf16[192,4096]{1,0:T(8,128)(2,1)} %convolution_convert_fusion.part, bf16[192,512]{1,0:T(8,128)(2,1)} %dynamic_slice.3.base, f32[192,512]{1,0:T(8,128)} %get-tuple-element.9.mapped), custom_call_target="tpu_custom_call" | custom-call | tf_op jit(solution)/shard_map/pallas_call | solution.py:347
  193.9 0.0 copy-start.1
  193.9 0.0 copy-start.7
  193.9 3.4 %fusion.30 = f32[256,4096]{1,0:T(8,128)S(1)} fusion(bf16[384,4096]{1,0:T(8,128)(2,1)} %shard_map.138, f32[384,256]{1,0:T(8,128)} %copy-done.6, f32[256]{0:T(256)S(1)} %bitcast.38), kind=kOutput, calls=%fused_computation.44 | convolution fusion | flops 805502976 | bytes 7734272 | tf_op jit(solution)/shard_map/dot_general | solution.py:22
  197.3 0.0 copy-done.1
  197.3 0.0 copy-done.7
  197.4 2.8 %multiply_reduce_fusion = (f32[256]{0:T(256)S(1)}, f32[256]{0:T(256)S(1)}, f32[384,256]{1,0:T(8,128)S(1)}) fusion(f32[384,256]{1,0:T(8,128)S(1)} %copy-done.7, f32[256]{0:T(256)S(1)} %bitcast.39, bf16[384,4096]{1,0:T(8,128)(2,1)S(1)} %copy-done.1, bf16[256,4096]{1,0:T(8,128)(2,1)} %collective-permute-done.1), kind=kOutput, calls=%fused_computation.31 | convolution fusion | flops 805993984 | bytes 6032384 | tf_op jit(solution)/shard_map/dot_general | solution.py:16
  200.2 1.3 convolution_add_fusion
  201.5 3.8 %collective-permute-start.2 = (f32[256,4096]{1,0:T(8,128)S(1)}, f32[256,4096]{1,0:T(8,128)S(1)}, u32[]{:S(2)}, u32[]{:S(2)}) collective-permute-start(f32[256,4096]{1,0:T(8,128)S(1)} %convolution_add_fusion), channel_id=1, source_target_pairs={{0,1},{1,0},{2,3},{3,2},{4,5},{5,4},{6,7},{7,6},{8,9},{9,8},{10,11... | collective-permute-start | bytes 12582920 | tf_op jit(solution)/shard_map/ppermute | solution.py:405
  205.3 0.1 collective-permute-start.3
  205.4 0.0 copy-start.4
  205.4 2.8 %multiply_reduce_fusion.1 = (f32[256]{0:T(256)S(1)}, f32[256]{0:T(256)S(1)}, f32[384,256]{1,0:T(8,128)S(1)}) fusion(f32[384,256]{1,0:T(8,128)S(1)} %fusion.14, f32[256]{0:T(256)S(1)} %bitcast.34, bf16[384,4096]{1,0:T(8,128)(2,1)S(1)} %copy-done.1, bf16[256,4096]{1,0:T(8,128)(2,1)} %convert_element_type.38), kind=kOutput, calls=%fused_computation.32 | convolution fusion | flops 805993984 | bytes 6032384 | tf_op jit(solution)/shard_map/dot_general | solution.py:16
  208.2 0.0 copy-start.11
  208.2 0.0 copy-start.12
  208.2 0.0 copy-start.3
  208.2 1.3 fusion.28
  209.5 2.6 %collective-permute-done.3 = f32[2,256]{1,0:T(2,128)S(1)} collective-permute-done((f32[2,256]{1,0:T(2,128)S(1)}, f32[2,256]{1,0:T(2,128)S(1)}, u32[]{:S(2)}, u32[]{:S(2)}) %collective-permute-start.3) | collective-permute-done | bytes 2080 | tf_op jit(solution)/shard_map/ppermute | solution.py:406
  212.1 0.0 copy-done.11
  212.1 0.0 copy-done.12
  212.1 0.6 divide_subtract_fusion.1
  212.7 0.6 pad_maximum_fusion.1
  213.3 0.0 collective-permute-done.2
  213.3 0.0 copy-start.5
  213.3 2.0 copy-done.5
  215.3 0.0 copy-done.4
  215.3 0.0 copy-done.3
  215.3 9.3 %divide_subtract_fusion = (f32[256,4096]{1,0:T(8,128)}, f32[256,4096]{1,0:T(8,128)}, f32[256,4096]{1,0:T(8,128)}) fusion(f32[256,4096]{1,0:T(8,128)S(1)} %copy-done.3, f32[256,4096]{1,0:T(8,128)S(1)} %copy-done.4, f32[256,4096]{1,0:T(8,128)} %param.15, f32[256,4096]{1,0:T(8,128)} %copy-done.5, f32[256,4096]{1,0:T(8,128)S(1)} %fusion.28, ...), kind=kOutput, calls=%fused_computation.5 | convolution fusion | flops 821526528 | bytes 37487616 | tf_op jit(solution)/shard_map/dot_general | solution.py:22
  (5 shorter events, 0.0 us)
Async XLA Ops:
  0.6 4.5 %copy-start.9 = (f32[2,256]{1,0:T(2,128)S(1)}, f32[2,256]{1,0:T(2,128)}, u32[]{:S(2)}) copy-start(f32[2,256]{1,0:T(2,128)} %param.13) | copy-start | bytes 6148
  0.6 39.1 %copy-start.8 = (f32[2,1024]{1,0:T(2,128)S(1)}, f32[2,1024]{1,0:T(2,128)}, u32[]{:S(2)}) copy-start(f32[2,1024]{1,0:T(2,128)} %param.11) | copy-start | bytes 24580
  4.5 45.6 %collective-permute-start.1 = (bf16[256,4096]{1,0:T(8,128)(2,1)}, bf16[256,4096]{1,0:T(8,128)(2,1)}, u32[]{:S(2)}, u32[]{:S(2)}) collective-permute-start(bf16[256,4096]{1,0:T(8,128)(2,1)} %convert_element_type.38), channel_id=1, source_target_pairs={{0,1},{1,0},{2,3},{3,2},{4,5},{5,4},{6,7},{7,6},{8,9},{9,8},{10,11... | collective-permute-start | bytes 6291464 | tf_op jit(solution)/shard_map/ppermute | solution.py:378
  5.1 44.9 %collective-permute-start = (bf16[2,256]{1,0:T(2,128)(2,1)S(1)}, bf16[2,256]{1,0:T(2,128)(2,1)S(1)}, u32[]{:S(2)}, u32[]{:S(2)}) collective-permute-start(bf16[2,256]{1,0:T(2,128)(2,1)S(1)} %convert_element_type.37), channel_id=1, source_target_pairs={{0,1},{1,0},{2,3},{3,2},{4,5},{5,4},{6,7},{7,6},{8,9},{9,8},{10,11... | collective-permute-start | bytes 3080 | tf_op jit(solution)/shard_map/ppermute | solution.py:379
  43.9 5.4 %copy-start = (bf16[16,24,4096]{2,1,0:T(8,128)(2,1)S(1)}, bf16[16,24,4096]{2,1,0:T(8,128)(2,1)}, u32[]{:S(2)}) copy-start(bf16[16,24,4096]{2,1,0:T(8,128)(2,1)} %shard_map.136) | copy-start | bytes 9437188
  49.3 4.5 %copy-start.2 = (f32[384,4096]{1,0:T(8,128)S(1)}, f32[384,4096]{1,0:T(8,128)}, u32[]{:S(2)}) copy-start(f32[384,4096]{1,0:T(8,128)} %fusion.29) | copy-start | bytes 18874372
  53.0 0.7 copy-start.6
  53.8 73.3 %copy-start.10 = (f32[1,1024]{1,0:T(1,128)S(1)}, f32[1,1024]{1,0:T(1,128)}, u32[]{:S(2)}) copy-start(f32[1,1024]{1,0:T(1,128)} %get-tuple-element.20) | copy-start | bytes 12292
  193.9 3.5 %copy-start.1 = (bf16[384,4096]{1,0:T(8,128)(2,1)S(1)}, bf16[384,4096]{1,0:T(8,128)(2,1)}, u32[]{:S(2)}) copy-start(bf16[384,4096]{1,0:T(8,128)(2,1)} %shard_map.138) | copy-start | bytes 9437188
  193.9 3.5 %copy-start.7 = (f32[384,256]{1,0:T(8,128)S(1)}, f32[384,256]{1,0:T(8,128)}, u32[]{:S(2)}) copy-start(f32[384,256]{1,0:T(8,128)} %copy-done.6) | copy-start | bytes 1179652
  201.5 11.7 %collective-permute-start.2 = (f32[256,4096]{1,0:T(8,128)S(1)}, f32[256,4096]{1,0:T(8,128)S(1)}, u32[]{:S(2)}, u32[]{:S(2)}) collective-permute-start(f32[256,4096]{1,0:T(8,128)S(1)} %convolution_add_fusion), channel_id=1, source_target_pairs={{0,1},{1,0},{2,3},{3,2},{4,5},{5,4},{6,7},{7,6},{8,9},{9,8},{10,11... | collective-permute-start | bytes 12582920 | tf_op jit(solution)/shard_map/ppermute | solution.py:405
  205.3 6.8 %collective-permute-start.3 = (f32[2,256]{1,0:T(2,128)S(1)}, f32[2,256]{1,0:T(2,128)S(1)}, u32[]{:S(2)}, u32[]{:S(2)}) collective-permute-start(f32[2,256]{1,0:T(2,128)S(1)} %pad_maximum_fusion), channel_id=1, source_target_pairs={{0,1},{1,0},{2,3},{3,2},{4,5},{5,4},{6,7},{7,6},{8,9},{9,8},{10,11... | collective-permute-start | bytes 6152 | tf_op jit(solution)/shard_map/ppermute | solution.py:406
  205.4 9.9 %copy-start.4 = (f32[256,4096]{1,0:T(8,128)S(1)}, f32[256,4096]{1,0:T(8,128)}, u32[]{:S(2)}) copy-start(f32[256,4096]{1,0:T(8,128)} %param.14) | copy-start | bytes 12582916
  208.2 3.9 %copy-start.11 = (f32[2,256]{1,0:T(2,128)S(1)}, f32[2,256]{1,0:T(2,128)}, u32[]{:S(2)}) copy-start(f32[2,256]{1,0:T(2,128)} %param.16) | copy-start | bytes 6148
  208.2 3.9 %copy-start.12 = (f32[2,256]{1,0:T(2,128)S(1)}, f32[2,256]{1,0:T(2,128)}, u32[]{:S(2)}) copy-start(f32[2,256]{1,0:T(2,128)} %param.17) | copy-start | bytes 6148
  208.2 7.1 %copy-start.3 = (f32[256,4096]{1,0:T(8,128)S(1)}, f32[256,4096]{1,0:T(8,128)}, u32[]{:S(2)}) copy-start(f32[256,4096]{1,0:T(8,128)} %param.12) | copy-start | bytes 12582916
  213.3 2.0 copy-start.5

commit v3 on v2

--- a/solution.py
+++ b/solution.py
@@ -78,67 +78,89 @@
             copy.wait_send()
 
 
-def gather_line(sender, view, z, x, y, z_peers, x_peer, y_peer, own):
-    here = view(z, x, y)
-    to_z = [sender.send(own, here, peer) for peer in z_peers]
-    over_x, over_y = [sender.send(own, here, x_peer)], []
-    if y_peer is not None:
-        over_y.append(sender.send(own, here, y_peer))
-    for k in (1, 3, 2):
-        source = lax.rem(z + 4 - k, 4)
-        to_z[k - 1].wait_recv()
-        block = view(source, x, y)
-        over_x.append(sender.send(block, block, x_peer))
-        if y_peer is not None:
-            over_y.append(sender.send(block, block, y_peer))
-    return over_x, over_y
-
-
-def gather_all(sender, view, half, z, x, y, z_peers, x_peer, y_peer, own):
-    over_x, over_y = gather_line(sender, view, z, x, y, z_peers, x_peer, y_peer, own)
+def gather_steps(sender, view, top, bottom, spot, source_ref=None):
+    z, x, y, z_peers, x_peer, y_peer = spot
+    place_own = view(z, x, y)
+    own = place_own if source_ref is None else source_ref
+    to_line = [sender.send(own, place_own, z_peers[k - 1]) for k in (1, 2, 3)]
+    over_x, over_y = [sender.send(own, place_own, x_peer)], [sender.send(own, place_own, y_peer)]
     diagonal = []
-    for i, k in enumerate((0, 1, 3, 2)):
-        source = lax.rem(z + 4 - k, 4)
+    yield
+
+    def cross(i):
+        source = lax.rem(z + 4 - ARRIVAL[i], 4)
         over_x[i].wait_recv()
-        block = half(source, 1 - x, y, 0)
+        block = top(source, 1 - x, y)
         diagonal.append(sender.send(block, block, y_peer))
         over_y[i].wait_recv()
-        block = half(source, x, 1 - y, 1)
+        block = bottom(source, x, 1 - y)
         diagonal.append(sender.send(block, block, x_peer))
+
+    for i, k in enumerate(ARRIVAL):
+        if i:
+            to_line[k - 1].wait_recv()
+            block = view(lax.rem(z + 4 - k, 4), x, y)
+            over_x.append(sender.send(block, block, x_peer))
+            over_y.append(sender.send(block, block, y_peer))
+            yield
+            cross(i - 1)
+            yield
+    cross(3)
+    yield
     for copy in diagonal:
         copy.wait_recv()
-
-
-def gather_kernel(own_ref, all_ref, send_sem, recv_sem, local_sem):
-    z, x, y, z_peers, x_peer, y_peer = place()
+    yield
+
+
+def gather_kernel(own_ref, weight_ref, all_ref, weight_own, weight_other, wide, send_sem, recv_sem, local_sem):
+    spot = place()
+    z, x, y, z_peers, x_peer, y_peer = spot
     width = own_ref.shape[1] // 2
     view = lambda zz, xx, yy: all_ref.at[yy * 8 + zz * 2 + xx]
-    half = lambda zz, xx, yy, h: all_ref.at[yy * 8 + zz * 2 + xx, :, pl.ds(h * width, width)]
-    greet(z_peers + [x_peer, y_peer])
-    local = pltpu.make_async_copy(own_ref, view(z, x, y), local_sem)
+    top = lambda zz, xx, yy: all_ref.at[yy * 8 + zz * 2 + xx, :, pl.ds(0, width)]
+    bottom = lambda zz, xx, yy: all_ref.at[yy * 8 + zz * 2 + xx, :, pl.ds(width, width)]
+    fsdp, rep = x_peer[0] + 2 * x - 1, x_peer[1]
+    partner = (fsdp, rep + 1 - 2 * lax.rem(rep, 2))
+    local = pltpu.make_async_copy(own_ref, view(z, x, y), local_sem.at[0])
     local.start()
+    load = pltpu.make_async_copy(weight_ref, wide, local_sem.at[1])
+    load.start()
+    greet(z_peers + [x_peer, y_peer, partner])
     sender = Sender(send_sem, recv_sem)
-    gather_all(sender, view, half, z, x, y, z_peers, x_peer, y_peer, own_ref)
+    steps = gather_steps(sender, view, top, bottom, spot, own_ref)
+    next(steps)
+    load.wait()
+    weight_own[...] = wide[...].astype(BF16)
+    swapped = sender.send(weight_own, weight_other, partner)
+    for _ in steps:
+        pass
+    swapped.wait_recv()
+    local.wait()
     sender.drain()
-    local.wait()
-
-
-def gather_samples(samples):
+
+
+def gather_samples(samples, weight):
     rows, width = samples.shape
-    gathered = pl.pallas_call(
+    low = jax.ShapeDtypeStruct(weight.shape, BF16)
+    gathered, own, other = pl.pallas_call(
         gather_kernel,
-        out_shape=jax.ShapeDtypeStruct((16, rows, width), samples.dtype),
-        in_specs=[pl.BlockSpec(memory_space=pl.ANY)],
-        out_specs=pl.BlockSpec(memory_space=pl.ANY),
+        out_shape=(jax.ShapeDtypeStruct((16, rows, width), samples.dtype), low, low),
+        in_specs=[pl.BlockSpec(memory_space=pl.ANY)] * 2,
+        out_specs=[
+            pl.BlockSpec(memory_space=pl.ANY),
+            pl.BlockSpec(memory_space=pltpu.VMEM),
+            pl.BlockSpec(memory_space=pltpu.VMEM),
+        ],
         scratch_shapes=[
-            pltpu.SemaphoreType.DMA((19,)),
-            pltpu.SemaphoreType.DMA((19,)),
-            pltpu.SemaphoreType.DMA,
+            pltpu.VMEM(weight.shape, F32),
+            pltpu.SemaphoreType.DMA((20,)),
+            pltpu.SemaphoreType.DMA((20,)),
+            pltpu.SemaphoreType.DMA((2,)),
         ],
         compiler_params=pltpu.CompilerParams(collective_id=1, has_side_effects=True),
         cost_estimate=pl.CostEstimate(flops=0, bytes_accessed=100_000_000, transcendentals=0),
-    )(samples)
-    return gathered.reshape(16 * rows, width)
+    )(samples, weight)
+    return gathered.reshape(16 * rows, width), (own, other)
 
 
 ORDER = (2, 1, 3, 0)
@@ -152,7 +174,7 @@
 
 
 def map_steps(
-    chunk, sender, spot, cut, part, base, mapped, low, from_y, from_x, to_x, to_y, late_x, late_y, to_z, from_z
+    chunk, sender, spot, cut, fill, part, base, mapped, low, from_y, from_x, to_x, to_y, late_x, late_y, to_z, from_z
 ):
     z, x, y, z_peers, x_peer, y_peer = spot
     rows, width = base.shape
@@ -169,6 +191,8 @@
     for k in ORDER:
         zz = lax.rem(z + k, 4)
         pair = pl.ds(pl.multiple_of(zz * 2 * width, 2 * width), 2 * width)
+        if chunk == 0:
+            fill(k, pair)
         first_y[k] = sender.send(part.at[top_rows(1 - y), pair], from_y.at[k], y_peer)
         first_x[k] = [
             sender.send(part.at[low_rows(yy), cols(zz, 1 - x)], from_x.at[k, yy], x_peer) for yy in (0, 1)
@@ -229,18 +253,44 @@
 MAP_SCHEDULE = [0] * 4 + [0, 1] * 8 + [0, 1, 1, 0, 1, 0, 1, 0, 1, 1, 1, 1, 1, 0]
 
 
-def map_kernel(part, base, mapped, low, *rest):
-    scratch, (send_sem, recv_sem) = rest[:-2], rest[-2:]
+def stream_columns(z, pairs, local_sem, width):
+    loads = {}
+    for k in ORDER:
+        span = pl.ds(pl.multiple_of(lax.rem(z + k, 4) * width, width), width)
+        loads[k] = [
+            pltpu.make_async_copy(source.at[:, span], held.at[k], local_sem.at[i, k])
+            for i, (source, held) in enumerate(pairs)
+        ]
+        for load in loads[k]:
+            load.start()
+    return loads
+
+
+def map_kernel(left_own, left_other, weight_own, weight_other, base, mapped, low, *rest):
+    part, held_own, held_other = rest[:3]
+    scratch, (send_sem, recv_sem, local_sem) = rest[3:-3], rest[-3:]
     spot = place()
+    loads = stream_columns(
+        spot[0], ((weight_own, held_own), (weight_other, held_other)), local_sem, held_own.shape[2]
+    )
+
+    def fill(k, pair):
+        for load in loads[k]:
+            load.wait()
+        part[:, pair] = (
+            jnp.dot(left_own[...], held_own[k], preferred_element_type=F32)
+            + jnp.dot(left_other[...], held_other[k], preferred_element_type=F32)
+        ).astype(BF16)
+
     greet(spot[3] + list(spot[4:]))
     sender = Sender(send_sem, recv_sem)
     cut = scratch[2].shape[2]
-    steps = [map_steps(c, sender, spot, cut, part, base, mapped, low, *scratch) for c in range(CHUNKS)]
+    steps = [map_steps(c, sender, spot, cut, fill, part, base, mapped, low, *scratch) for c in range(CHUNKS)]
     interleave(steps[0], steps[1], MAP_SCHEDULE)
     sender.drain()
 
 
-def reduce_map(part, base):
+def reduce_map(lefts, weights, base):
     rows, width = base.shape
     span = rows // CHUNKS
     cut = span // 3 * 2
@@ -248,11 +298,20 @@
         map_kernel,
         out_shape=(
             jax.ShapeDtypeStruct((rows, width), F32),
-            jax.ShapeDtypeStruct((rows, part.shape[1]), BF16),
+            jax.ShapeDtypeStruct((rows, 8 * width), BF16),
         ),
-        in_specs=[pl.BlockSpec(memory_space=pltpu.VMEM)] * 2,
+        in_specs=[
+            pl.BlockSpec(memory_space=pltpu.VMEM),
+            pl.BlockSpec(memory_space=pltpu.VMEM),
+            pl.BlockSpec(memory_space=pl.ANY),
+            pl.BlockSpec(memory_space=pl.ANY),
+            pl.BlockSpec(memory_space=pltpu.VMEM),
+        ],
         out_specs=[pl.BlockSpec(memory_space=pltpu.VMEM)] * 2,
         scratch_shapes=[
+            pltpu.VMEM((2 * rows, 8 * width), BF16),
+            pltpu.VMEM((4, weights[0].shape[0], 2 * width), BF16),
+            pltpu.VMEM((4, weights[1].shape[0], 2 * width), BF16),
             pltpu.VMEM((CHUNKS, 4, cut, 2 * width), BF16),
             pltpu.VMEM((CHUNKS, 4, 2, span - cut, width), BF16),
             pltpu.VMEM((CHUNKS, 4, cut, width), BF16),
@@ -263,12 +322,13 @@
             pltpu.VMEM((CHUNKS, 3, span, width), BF16),
             pltpu.SemaphoreType.DMA((30 * CHUNKS,)),
             pltpu.SemaphoreType.DMA((30 * CHUNKS,)),
+            pltpu.SemaphoreType.DMA((2, 4)),
         ],
         compiler_params=pltpu.CompilerParams(collective_id=2, has_side_effects=True),
-    )(part, base)
-
-
-def dual_steps(chunk, sender, spot, part, base, mapped, full, from_x, to_z, from_z):
+    )(*lefts, *weights, base)
+
+
+def dual_steps(chunk, sender, spot, fill, part, base, mapped, full, from_x, to_z, from_z):
     z, x, y, z_peers, x_peer, y_peer = spot
     rows, width = base.shape
     span = rows // CHUNKS
@@ -285,6 +345,8 @@
     from_x, to_z, from_z = (ref.at[chunk] for ref in (from_x, to_z, from_z))
     first, third = {}, {}
     for k in ORDER:
+        if chunk == 0:
+            fill(k, pl.ds(pl.multiple_of(lax.rem(z + k, 4) * 2 * width, 2 * width), 2 * width))
         first[k] = sender.send(part.at[here, cols(lax.rem(z + k, 4), 1 - x)], from_x.at[k], x_peer)
         yield
     for k in ORDER:
@@ -302,62 +364,54 @@
     full[pl.ds(pl.multiple_of(y * rows + chunk * span, 16), span), cols(z, x)] = (
         base[here].astype(F32) - grad
     ).astype(BF16)
-    own = view(z, x, y)
-    to_line = [sender.send(own, own, peer) for peer in z_peers]
-    over_x, over_y = [sender.send(own, own, x_peer)], [sender.send(own, own, y_peer)]
-    yield
-    for k in ARRIVAL[1:]:
-        to_line[k - 1].wait_recv()
-        block = view(lax.rem(z + 4 - k, 4), x, y)
-        over_x.append(sender.send(block, block, x_peer))
-        over_y.append(sender.send(block, block, y_peer))
-        yield
-    diagonal = []
-    for i, k in enumerate(ARRIVAL):
-        source = lax.rem(z + 4 - k, 4)
-        over_x[i].wait_recv()
-        block = top(source, 1 - x, y)
-        diagonal.append(sender.send(block, block, y_peer))
-        over_y[i].wait_recv()
-        block = bottom(source, x, 1 - y)
-        diagonal.append(sender.send(block, block, x_peer))
-        yield
-    for copy in diagonal:
-        copy.wait_recv()
-    yield
+    yield from gather_steps(sender, view, top, bottom, spot)
 
 
 DUAL_SCHEDULE = [0] * 4 + [0, 1] * 4 + [0, 1, 0, 1, 0, 1, 0, 1, 1] + [0, 1] * 3 + [0] + [1] * 4 + [0, 1]
 
 
-def dual_kernel(part, base, mapped, full, from_x, to_z, from_z, send_sem, recv_sem):
+def dual_kernel(left, weight, base, mapped, full, part, held, from_x, to_z, from_z, send_sem, recv_sem, local_sem):
     spot = place()
+    loads = stream_columns(spot[0], ((weight, held),), local_sem, held.shape[2])
+
+    def fill(k, pair):
+        loads[k][0].wait()
+        part[:, pair] = jnp.dot(left[...], held[k], preferred_element_type=F32).astype(BF16)
+
     greet(spot[3] + list(spot[4:]))
     sender = Sender(send_sem, recv_sem)
     steps = [
-        dual_steps(c, sender, spot, part, base, mapped, full, from_x, to_z, from_z) for c in range(CHUNKS)
+        dual_steps(c, sender, spot, fill, part, base, mapped, full, from_x, to_z, from_z) for c in range(CHUNKS)
     ]
     interleave(steps[0], steps[1], DUAL_SCHEDULE)
     sender.drain()
 
 
-def reduce_dual(part, base, mapped):
+def reduce_dual(left, weight, base, mapped):
     rows, width = base.shape
     span = rows // CHUNKS
     return pl.pallas_call(
         dual_kernel,
-        out_shape=jax.ShapeDtypeStruct((2 * rows, part.shape[1]), BF16),
-        in_specs=[pl.BlockSpec(memory_space=pltpu.VMEM)] * 3,
+        out_shape=jax.ShapeDtypeStruct((2 * rows, weight.shape[1]), BF16),
+        in_specs=[
+            pl.BlockSpec(memory_space=pltpu.VMEM),
+            pl.BlockSpec(memory_space=pl.ANY),
+            pl.BlockSpec(memory_space=pltpu.VMEM),
+            pl.BlockSpec(memory_space=pltpu.VMEM),
+        ],
         out_specs=pl.BlockSpec(memory_space=pltpu.VMEM),
         scratch_shapes=[
+            pltpu.VMEM((rows, 8 * width), BF16),
+            pltpu.VMEM((4, weight.shape[0], 2 * width), BF16),
             pltpu.VMEM((CHUNKS, 4, span, width), BF16),
             pltpu.VMEM((CHUNKS, 3, span, width), BF16),
             pltpu.VMEM((CHUNKS, 3, span, width), BF16),
             pltpu.SemaphoreType.DMA((26 * CHUNKS,)),
             pltpu.SemaphoreType.DMA((26 * CHUNKS,)),
+            pltpu.SemaphoreType.DMA((1, 4)),
         ],
         compiler_params=pltpu.CompilerParams(collective_id=3, has_side_effects=True),
-    )(part, base, mapped)
+    )(left, weight, base, mapped)
 
 
 def chip_body(
@@ -373,28 +427,21 @@
 ):
     swap = [(0, 1), (1, 0), (2, 3), (3, 2)]
     fsdp, rep = lax.axis_index("fsdp"), lax.axis_index("rep")
-    weight = map_weight.astype(BF16)
     vector = map_vector.astype(BF16)
-    weights = (weight, lax.ppermute(weight, "rep", swap))
     vectors = (vector, lax.ppermute(vector, "rep", swap))
-    rows = gather_samples(samples)
+    rows, weights = gather_samples(samples, map_weight)
     inverse_rows = 1.0 / (rows.shape[0] * 2)
     sigmas, scales = [], []
     for block, pair in zip(weights, vectors):
         sigma = jax.nn.sigmoid(contract_last(rows, block) + pair[1].astype(F32))
         sigmas.append(sigma)
         scales.append((pair[0].astype(F32) * sigma).astype(BF16))
-    part = (
-        jnp.dot(scales[0], weights[0], preferred_element_type=F32)
-        + jnp.dot(scales[1], weights[1], preferred_element_type=F32)
-    ).astype(BF16)
     half, width = rows.shape[0] // 2, rows.shape[1] // 8
     base = lax.dynamic_slice(rows, ((rep // 2) * half, fsdp * width), (half, width))
-    mapped, mapped_low = reduce_map(part, base)
+    mapped, mapped_low = reduce_map(scales, weights, base)
     dual_hidden = contract_last(mapped_low, dual_weight) + dual_vector[1]
     dual_scaled = (dual_vector[0] * jax.nn.sigmoid(dual_hidden)).astype(BF16)
-    dual_part = jnp.dot(dual_scaled, dual_weight, preferred_element_type=F32).astype(BF16)
-    residual = reduce_dual(dual_part, base, mapped)
+    residual = reduce_dual(dual_scaled, dual_weight, base, mapped)
     grads, smalls = [], []
     for block, pair, sigma, scaled in zip(weights[::-1], vectors[::-1], sigmas[::-1], scales[::-1]):
         readout = pair[0].astype(F32)

time: 225 us -> 210 us (0.933)
  matrix products: 49.1 us -> 33.1 us
  starting transfers between devices: 4.59 us -> 8.59 us
  other arithmetic: 5.01 us -> 1.89 us
    dot_general x3 -> x0, matrix products: 21.6 us -> none  [the longest x1 12 us: chip_body(): jnp.dot(dual_scaled, dual_weight, preferred_element_type=F32).astype(BF16)]
    dot_general x4 -> x5, matrix products: 12.1 us -> 17.8 us  [contract_last(): lax.dot_general(left, right, (((1,), (1,)), ((), ())), preferred_element_...]
    ppermute x1, starting transfers between devices: 3.76 us -> 7.83 us  [chip_body(): lax.ppermute(grads[0], 'rep', swap)]
    convert_element_type x1 -> x0, other arithmetic: 3.8 us -> none  [chip_body(): weight = map_weight.astype(BF16)]
  transfers between devices with their start and end apart: 4 -> 3, of which waited for: 1 -> 1; matrix products, arithmetic and copies ran while one was open for 7% -> 5% of each run, Pallas kernels for 15% -> 17%
where the time goes in v3:
time: 210 us; the launch traced here: 209 us
  Pallas kernels  157 us (75%)
  matrix products  33.1 us (16%)
  starting transfers between devices  8.59 us (4%)
  waiting for transfers between devices  4.33 us (2%)
  local copies, waits for them, and re-layouts  3.68 us (2%)
    pallas_call x1, Pallas kernels, reduce_map(): pl.pallas_call(map_kernel, out_shape=(jax.ShapeDtypeStruct((rows, width),...  67.4 us
    pallas_call x1, Pallas kernels, reduce_dual(): pl.pallas_call(dual_kernel, out_shape=jax.ShapeDtypeStruct((2 * rows, wei...  53.9 us
    pallas_call x1, Pallas kernels, gather_samples(): pl.pallas_call(gather_kernel, out_shape=(jax.ShapeDtypeStruct((16, rows,...  35.3 us
    dot_general x5, matrix products, contract_last(): lax.dot_general(left, right, (((1,), (1,)), ((), ())), preferred_element_...  17.8 us
    dot_general x4, matrix products, contract_first(): lax.dot_general(left, right, (((0,), (0,)), ((), ())), preferred_element_...  15.3 us
    ppermute x1, starting transfers between devices, chip_body(): lax.ppermute(grads[0], 'rep', swap)  7.83 us
    ppermute x1, waiting for transfers between devices, chip_body(): lax.ppermute(smalls[0], 'rep', swap)  4.33 us
  transfers between devices with their start and end apart: 3, of which 1 were waited for; matrix products, arithmetic and copies ran while one was open for 5% of the time, Pallas kernels for 17%

profile of v3, /device:TPU:17, one launch (start us, length us, event | category | flops | bytes accessed | tf_op | source)
XLA Modules:
  0.0 209.0 jit_solution(16296588739107664105)
XLA Ops:
  0.6 0.7 convert_element_type.28
  1.3 0.7 collective-permute-start
  2.0 0.8 fusion.23
  2.8 35.3 %shard_map.136 = (bf16[16,24,4096]{2,1,0:T(8,128)(2,1)}, bf16[256,4096]{1,0:T(8,128)(2,1)}, bf16[256,4096]{1,0:T(8,128)(2,1)}) custom-call(bf16[24,4096]{1,0:T(8,128)(2,1)} %own_ref.1, f32[256,4096]{1,0:T(8,128)} %weight_ref.1), custom_call_target="tpu_custom_call" | custom-call | bytes 100000000 | tf_op jit(solution)/shard_map/pallas_call | solution.py:145
  38.1 0.0 copy-start.2
  38.1 4.5 %multiply_convert_fusion.1 = (bf16[384,256]{1,0:T(8,128)(2,1)}, f32[384,256]{1,0:T(8,128)}) fusion(f32[256]{0:T(256)S(1)} %bitcast.38, f32[256]{0:T(256)S(1)} %bitcast.45, bf16[384,4096]{1,0:T(8,128)(2,1)} %bitcast.27, bf16[256,4096]{1,0:T(8,128)(2,1)} %get-tuple-element.12.weight_own), kind=kOutput, calls=%fused_computation.28 | convolution fusion | flops 805896192 | bytes 5834752 | tf_op jit(solution)/shard_map/dot_general | solution.py:16
  42.7 0.0 copy-done.2
  42.7 0.7 dynamic_slice.3.base
  43.4 0.0 collective-permute-done
  43.4 3.4 %multiply_convert_fusion = (bf16[384,256]{1,0:T(8,128)(2,1)}, f32[384,256]{1,0:T(8,128)}) fusion(f32[256]{0:T(256)S(1)} %bitcast.35, f32[256]{0:T(256)S(1)} %bitcast.32, bf16[384,4096]{1,0:T(8,128)(2,1)S(1)} %bitcast.29, bf16[256,4096]{1,0:T(8,128)(2,1)} %get-tuple-element.13.weight_other), kind=kOutput, calls=%fused_computation.26 | convolution fusion | flops 805896192 | bytes 5834752 | tf_op jit(solution)/shard_map/dot_general | solution.py:16
  46.8 67.4 %shard_map.137 = (f32[192,512]{1,0:T(8,128)}, bf16[192,4096]{1,0:T(8,128)(2,1)}) custom-call(bf16[384,256]{1,0:T(8,128)(2,1)} %get-tuple-element.36.left_own, bf16[384,256]{1,0:T(8,128)(2,1)} %get-tuple-element.34.left_other, bf16[256,4096]{1,0:T(8,128)(2,1)} %get-tuple-element.12.weight_own, bf16[256,4096]{1,0:T(8,128)(2,1)} %get-tuple-element.13.weight_other, ...), custom_call_target="tpu_custom_call" | custom-call | tf_op jit(solution)/shard_map/pallas_call | solution.py:297
  114.2 7.6 %fusion.6.left = bf16[192,1024]{1,0:T(8,128)(2,1)} fusion(bf16[192,4096]{1,0:T(8,128)(2,1)} %get-tuple-element.14, bf16[1024,4096]{1,0:T(8,128)(2,1)} %weight.1, f32[1024]{0:T(1024)S(1)} %bitcast.42, f32[1024]{0:T(1024)S(1)} %bitcast.41), kind=kOutput, calls=%fused_computation.12 | convolution fusion | flops 1611792384 | bytes 10362880 | tf_op jit(solution)/shard_map/dot_general | solution.py:16
  121.8 0.0 copy-start.8
  121.8 53.9 %shard_map.138 = bf16[384,4096]{1,0:T(8,128)(2,1)} custom-call(bf16[192,1024]{1,0:T(8,128)(2,1)} %fusion.6.left, bf16[1024,4096]{1,0:T(8,128)(2,1)} %weight.1, bf16[192,512]{1,0:T(8,128)(2,1)} %dynamic_slice.3.base, f32[192,512]{1,0:T(8,128)} %get-tuple-element.15.mapped), custom_call_target="tpu_custom_call" | custom-call | tf_op jit(solution)/shard_map/pallas_call | solution.py:393
  175.7 0.0 copy-done.8
  175.7 0.0 copy-start
  175.7 0.0 copy-start.6
  175.7 0.0 copy-start.10
  175.7 3.3 %fusion.25 = f32[256,4096]{1,0:T(8,128)S(1)} fusion(bf16[384,256]{1,0:T(8,128)(2,1)S(1)} %copy-done.8, bf16[384,4096]{1,0:T(8,128)(2,1)} %shard_map.138), kind=kOutput, calls=%fused_computation.48 | convolution fusion | flops 805306368 | bytes 7536640 | tf_op jit(solution)/shard_map/dot_general | solution.py:22
  179.1 0.0 copy-done
  179.1 0.1 copy-done.6
  179.2 0.0 copy-done.10
  179.2 1.2 multiply_reduce_fusion
  180.4 0.0 copy-start.5
  180.4 0.0 copy-start.9
  180.4 1.4 convolution_add_fusion
  181.9 0.0 copy-start.7
  181.9 7.8 %collective-permute-start.1 = (f32[256,4096]{1,0:T(8,128)S(1)}, f32[256,4096]{1,0:T(8,128)S(1)}, u32[]{:S(2)}, u32[]{:S(2)}) collective-permute-start(f32[256,4096]{1,0:T(8,128)S(1)} %convolution_add_fusion), channel_id=1, source_target_pairs={{0,1},{1,0},{2,3},{3,2},{4,5},{5,4},{6,7},{7,6},{8,9},{9,8},{10,11... | collective-permute-start | bytes 12582920 | tf_op jit(solution)/shard_map/ppermute | solution.py:452
  189.7 0.1 collective-permute-start.2
  189.8 0.0 copy-done.5
  189.8 0.0 copy-done.9
  189.8 0.0 copy-start.3
  189.8 1.0 multiply_reduce_fusion.1
  190.8 0.0 copy-done.7
  190.8 0.0 copy-start.11
  190.8 0.0 copy-start.12
  190.9 0.0 copy-start.13
  190.9 0.0 copy-start.1
  190.9 1.3 fusion.24
  192.2 4.3 %collective-permute-done.2 = f32[2,256]{1,0:T(2,128)S(1)} collective-permute-done((f32[2,256]{1,0:T(2,128)S(1)}, f32[2,256]{1,0:T(2,128)S(1)}, u32[]{:S(2)}, u32[]{:S(2)}) %collective-permute-start.2) | collective-permute-done | bytes 2080 | tf_op jit(solution)/shard_map/ppermute | solution.py:453
  196.5 0.0 copy-done.11
  196.5 0.0 copy-done.12
  196.5 0.0 copy-done.13
  196.5 0.6 divide_subtract_fusion.1
  197.1 0.6 pad_maximum_fusion.1
  197.7 0.0 collective-permute-done.1
  197.7 0.0 copy-start.4
  197.7 2.0 copy-done.4
  199.7 0.0 copy-done.3
  199.7 0.0 copy-done.1
  199.7 9.3 %divide_subtract_fusion = (f32[256,4096]{1,0:T(8,128)}, f32[256,4096]{1,0:T(8,128)}, f32[256,4096]{1,0:T(8,128)}) fusion(f32[256,4096]{1,0:T(8,128)S(1)} %copy-done.1, f32[256,4096]{1,0:T(8,128)S(1)} %copy-done.3, f32[256,4096]{1,0:T(8,128)} %param.15, f32[256,4096]{1,0:T(8,128)} %copy-done.4, f32[256,4096]{1,0:T(8,128)S(1)} %fusion.24, ...), kind=kOutput, calls=%fused_computation.3 | convolution fusion | flops 821526528 | bytes 37487616 | tf_op jit(solution)/shard_map/dot_general | solution.py:22
  (4 shorter events, 0.0 us)
Async XLA Ops:
  1.3 42.1 %collective-permute-start = (bf16[2,256]{1,0:T(2,128)(2,1)S(1)}, bf16[2,256]{1,0:T(2,128)(2,1)S(1)}, u32[]{:S(2)}, u32[]{:S(2)}) collective-permute-start(bf16[2,256]{1,0:T(2,128)(2,1)S(1)} %convert_element_type.28), channel_id=1, source_target_pairs={{0,1},{1,0},{2,3},{3,2},{4,5},{5,4},{6,7},{7,6},{8,9},{9,8},{10,11... | collective-permute-start | bytes 3080 | tf_op jit(solution)/shard_map/ppermute | solution.py:431
  38.1 4.6 %copy-start.2 = (bf16[16,24,4096]{2,1,0:T(8,128)(2,1)S(1)}, bf16[16,24,4096]{2,1,0:T(8,128)(2,1)}, u32[]{:S(2)}) copy-start(bf16[16,24,4096]{2,1,0:T(8,128)(2,1)} %get-tuple-element.11) | copy-start | bytes 9437188
  121.8 53.9 %copy-start.8 = (bf16[384,256]{1,0:T(8,128)(2,1)S(1)}, bf16[384,256]{1,0:T(8,128)(2,1)}, u32[]{:S(2)}) copy-start(bf16[384,256]{1,0:T(8,128)(2,1)} %get-tuple-element.34.left_other) | copy-start | bytes 589828
  175.7 3.4 %copy-start = (bf16[384,4096]{1,0:T(8,128)(2,1)S(1)}, bf16[384,4096]{1,0:T(8,128)(2,1)}, u32[]{:S(2)}) copy-start(bf16[384,4096]{1,0:T(8,128)(2,1)} %shard_map.138) | copy-start | bytes 9437188
  175.7 3.5 %copy-start.6 = (bf16[256,4096]{1,0:T(8,128)(2,1)S(1)}, bf16[256,4096]{1,0:T(8,128)(2,1)}, u32[]{:S(2)}) copy-start(bf16[256,4096]{1,0:T(8,128)(2,1)} %get-tuple-element.13.weight_other) | copy-start | bytes 6291460
  175.7 3.5 %copy-start.10 = (f32[384,256]{1,0:T(8,128)S(1)}, f32[384,256]{1,0:T(8,128)}, u32[]{:S(2)}) copy-start(f32[384,256]{1,0:T(8,128)} %get-tuple-element.35) | copy-start | bytes 1179652
  180.4 9.4 %copy-start.5 = (bf16[256,4096]{1,0:T(8,128)(2,1)S(1)}, bf16[256,4096]{1,0:T(8,128)(2,1)}, u32[]{:S(2)}) copy-start(bf16[256,4096]{1,0:T(8,128)(2,1)} %get-tuple-element.12.weight_own) | copy-start | bytes 6291460
  180.4 9.4 %copy-start.9 = (f32[384,256]{1,0:T(8,128)S(1)}, f32[384,256]{1,0:T(8,128)}, u32[]{:S(2)}) copy-start(f32[384,256]{1,0:T(8,128)} %get-tuple-element.37) | copy-start | bytes 1179652
  181.9 9.0 %copy-start.7 = (bf16[384,256]{1,0:T(8,128)(2,1)S(1)}, bf16[384,256]{1,0:T(8,128)(2,1)}, u32[]{:S(2)}) copy-start(bf16[384,256]{1,0:T(8,128)(2,1)} %get-tuple-element.36.left_own) | copy-start | bytes 589828
  181.9 15.8 %collective-permute-start.1 = (f32[256,4096]{1,0:T(8,128)S(1)}, f32[256,4096]{1,0:T(8,128)S(1)}, u32[]{:S(2)}, u32[]{:S(2)}) collective-permute-start(f32[256,4096]{1,0:T(8,128)S(1)} %convolution_add_fusion), channel_id=1, source_target_pairs={{0,1},{1,0},{2,3},{3,2},{4,5},{5,4},{6,7},{7,6},{8,9},{9,8},{10,11... | collective-permute-start | bytes 12582920 | tf_op jit(solution)/shard_map/ppermute | solution.py:452
  189.7 6.8 %collective-permute-start.2 = (f32[2,256]{1,0:T(2,128)S(1)}, f32[2,256]{1,0:T(2,128)S(1)}, u32[]{:S(2)}, u32[]{:S(2)}) collective-permute-start(f32[2,256]{1,0:T(2,128)S(1)} %pad_maximum_fusion), channel_id=1, source_target_pairs={{0,1},{1,0},{2,3},{3,2},{4,5},{5,4},{6,7},{7,6},{8,9},{9,8},{10,11... | collective-permute-start | bytes 6152 | tf_op jit(solution)/shard_map/ppermute | solution.py:453
  189.8 9.9 %copy-start.3 = (f32[256,4096]{1,0:T(8,128)S(1)}, f32[256,4096]{1,0:T(8,128)}, u32[]{:S(2)}) copy-start(f32[256,4096]{1,0:T(8,128)} %param.14) | copy-start | bytes 12582916
  190.8 5.7 %copy-start.11 = (f32[2,256]{1,0:T(2,128)S(1)}, f32[2,256]{1,0:T(2,128)}, u32[]{:S(2)}) copy-start(f32[2,256]{1,0:T(2,128)} %param.13) | copy-start | bytes 6148
  190.8 5.6 %copy-start.12 = (f32[2,256]{1,0:T(2,128)S(1)}, f32[2,256]{1,0:T(2,128)}, u32[]{:S(2)}) copy-start(f32[2,256]{1,0:T(2,128)} %param.16) | copy-start | bytes 6148
  190.9 5.6 %copy-start.13 = (f32[2,256]{1,0:T(2,128)S(1)}, f32[2,256]{1,0:T(2,128)}, u32[]{:S(2)}) copy-start(f32[2,256]{1,0:T(2,128)} %param.17) | copy-start | bytes 6148
  190.9 8.8 %copy-start.1 = (f32[256,4096]{1,0:T(8,128)S(1)}, f32[256,4096]{1,0:T(8,128)}, u32[]{:S(2)}) copy-start(f32[256,4096]{1,0:T(8,128)} %weight_ref.1) | copy-start | bytes 12582916
  197.7 2.0 copy-start.4

commit v4 on v3

--- a/solution.py
+++ b/solution.py
@@ -293,7 +293,7 @@
 def reduce_map(lefts, weights, base):
     rows, width = base.shape
     span = rows // CHUNKS
-    cut = span // 3 * 2
+    cut = span // 6 * 5
     return pl.pallas_call(
         map_kernel,
         out_shape=(
@@ -332,7 +332,7 @@
     z, x, y, z_peers, x_peer, y_peer = spot
     rows, width = base.shape
     span = rows // CHUNKS
-    cut = span // 3 * 2
+    cut = span // 6 * 5
     cols = lambda zz, xx: pl.ds(pl.multiple_of((zz * 2 + xx) * width, width), width)
     here = slice(chunk * span, (chunk + 1) * span)
     view = lambda zz, xx, yy: full.at[

time: 210 us -> 218 us (1.038)
  Pallas kernels: 157 us -> 171 us
  starting transfers between devices: 8.59 us -> 2.33 us
    pallas_call x1, Pallas kernels: 53.9 us -> 64.4 us  [reduce_dual(): pl.pallas_call(dual_kernel, out_shape=jax.ShapeDtypeStruct((2 * rows, wei...]
    ppermute x1, starting transfers between devices: 7.83 us -> 1.57 us  [chip_body(): lax.ppermute(grads[0], 'rep', swap)]
    pallas_call x1, Pallas kernels: 67.4 us -> 71.6 us  [reduce_map(): pl.pallas_call(map_kernel, out_shape=(jax.ShapeDtypeStruct((rows, width),...]
  transfers between devices with their start and end apart: 3 -> 3, of which waited for: 1 -> 1; matrix products, arithmetic and copies ran while one was open for 5% -> 4% of each run, Pallas kernels for 17% -> 16%
where the time goes in v4:
time: 218 us
  Pallas kernels  171 us (78%)
  matrix products  33.1 us (15%)
  waiting for transfers between devices  4.33 us (2%)
  local copies, waits for them, and re-layouts  3.68 us (2%)
  starting transfers between devices  2.33 us (1%)
    pallas_call x1, Pallas kernels, reduce_map(): pl.pallas_call(map_kernel, out_shape=(jax.ShapeDtypeStruct((rows, width),...  71.6 us
    pallas_call x1, Pallas kernels, reduce_dual(): pl.pallas_call(dual_kernel, out_shape=jax.ShapeDtypeStruct((2 * rows, wei...  64.4 us
    pallas_call x1, Pallas kernels, gather_samples(): pl.pallas_call(gather_kernel, out_shape=(jax.ShapeDtypeStruct((16, rows,...  35.3 us
    dot_general x5, matrix products, contract_last(): lax.dot_general(left, right, (((1,), (1,)), ((), ())), preferred_element_...  17.8 us
    dot_general x4, matrix products, contract_first(): lax.dot_general(left, right, (((0,), (0,)), ((), ())), preferred_element_...  15.4 us
  transfers between devices with their start and end apart: 3, of which 1 were waited for; matrix products, arithmetic and copies ran while one was open for 4% of the time, Pallas kernels for 16%

profile of v4, /device:TPU:17, one launch (start us, length us, event | category | flops | bytes accessed | tf_op | source)
XLA Modules:
  0.0 217.6 jit_solution(2812552551887538310)
XLA Ops:
  0.6 0.7 convert_element_type.28
  1.3 0.7 collective-permute-start
  2.0 0.8 fusion.23
  2.8 35.3 %shard_map.136 = (bf16[16,24,4096]{2,1,0:T(8,128)(2,1)}, bf16[256,4096]{1,0:T(8,128)(2,1)}, bf16[256,4096]{1,0:T(8,128)(2,1)}) custom-call(bf16[24,4096]{1,0:T(8,128)(2,1)} %own_ref.1, f32[256,4096]{1,0:T(8,128)} %weight_ref.1), custom_call_target="tpu_custom_call" | custom-call | bytes 100000000 | tf_op jit(solution)/shard_map/pallas_call | solution.py:145
  38.1 0.0 copy-start.2
  38.1 4.5 %multiply_convert_fusion.1 = (bf16[384,256]{1,0:T(8,128)(2,1)}, f32[384,256]{1,0:T(8,128)}) fusion(f32[256]{0:T(256)S(1)} %bitcast.38, f32[256]{0:T(256)S(1)} %bitcast.45, bf16[384,4096]{1,0:T(8,128)(2,1)} %bitcast.27, bf16[256,4096]{1,0:T(8,128)(2,1)} %get-tuple-element.12.weight_own), kind=kOutput, calls=%fused_computation.28 | convolution fusion | flops 805896192 | bytes 5834752 | tf_op jit(solution)/shard_map/dot_general | solution.py:16
  42.7 0.0 copy-done.2
  42.7 0.7 dynamic_slice.3.base
  43.4 0.0 collective-permute-done
  43.4 3.4 %multiply_convert_fusion = (bf16[384,256]{1,0:T(8,128)(2,1)}, f32[384,256]{1,0:T(8,128)}) fusion(f32[256]{0:T(256)S(1)} %bitcast.35, f32[256]{0:T(256)S(1)} %bitcast.32, bf16[384,4096]{1,0:T(8,128)(2,1)S(1)} %bitcast.29, bf16[256,4096]{1,0:T(8,128)(2,1)} %get-tuple-element.13.weight_other), kind=kOutput, calls=%fused_computation.26 | convolution fusion | flops 805896192 | bytes 5834752 | tf_op jit(solution)/shard_map/dot_general | solution.py:16
  46.8 71.6 %shard_map.137 = (f32[192,512]{1,0:T(8,128)}, bf16[192,4096]{1,0:T(8,128)(2,1)}) custom-call(bf16[384,256]{1,0:T(8,128)(2,1)} %get-tuple-element.36.left_own, bf16[384,256]{1,0:T(8,128)(2,1)} %get-tuple-element.34.left_other, bf16[256,4096]{1,0:T(8,128)(2,1)} %get-tuple-element.12.weight_own, bf16[256,4096]{1,0:T(8,128)(2,1)} %get-tuple-element.13.weight_other, ...), custom_call_target="tpu_custom_call" | custom-call | tf_op jit(solution)/shard_map/pallas_call | solution.py:297
  118.4 7.6 %fusion.6.left = bf16[192,1024]{1,0:T(8,128)(2,1)} fusion(bf16[192,4096]{1,0:T(8,128)(2,1)} %get-tuple-element.14, bf16[1024,4096]{1,0:T(8,128)(2,1)} %weight.1, f32[1024]{0:T(1024)S(1)} %bitcast.42, f32[1024]{0:T(1024)S(1)} %bitcast.41), kind=kOutput, calls=%fused_computation.12 | convolution fusion | flops 1611792384 | bytes 10362880 | tf_op jit(solution)/shard_map/dot_general | solution.py:16
  126.0 0.0 copy-start.8
  126.0 64.4 %shard_map.138 = bf16[384,4096]{1,0:T(8,128)(2,1)} custom-call(bf16[192,1024]{1,0:T(8,128)(2,1)} %fusion.6.left, bf16[1024,4096]{1,0:T(8,128)(2,1)} %weight.1, bf16[192,512]{1,0:T(8,128)(2,1)} %dynamic_slice.3.base, f32[192,512]{1,0:T(8,128)} %get-tuple-element.15.mapped), custom_call_target="tpu_custom_call" | custom-call | tf_op jit(solution)/shard_map/pallas_call | solution.py:393
  190.5 0.0 copy-done.8
  190.5 0.0 copy-start
  190.5 0.0 copy-start.6
  190.5 0.0 copy-start.10
  190.5 3.3 %fusion.25 = f32[256,4096]{1,0:T(8,128)S(1)} fusion(bf16[384,256]{1,0:T(8,128)(2,1)S(1)} %copy-done.8, bf16[384,4096]{1,0:T(8,128)(2,1)} %shard_map.138), kind=kOutput, calls=%fused_computation.48 | convolution fusion | flops 805306368 | bytes 7536640 | tf_op jit(solution)/shard_map/dot_general | solution.py:22
  193.9 0.0 copy-done
  193.9 0.1 copy-done.6
  194.0 0.0 copy-done.10
  194.0 1.2 multiply_reduce_fusion
  195.2 0.0 copy-start.5
  195.2 0.0 copy-start.9
  195.2 1.4 convolution_add_fusion
  196.7 0.0 copy-start.7
  196.7 1.6 collective-permute-start.1
  198.3 0.1 collective-permute-start.2
  198.3 0.0 copy-done.5
  198.3 0.0 copy-done.9
  198.3 0.0 copy-start.3
  198.3 1.0 multiply_reduce_fusion.1
  199.4 0.0 copy-done.7
  199.4 0.0 copy-start.11
  199.4 0.0 copy-start.12
  199.4 0.0 copy-start.13
  199.4 0.0 copy-start.1
  199.4 1.3 fusion.24
  200.7 4.3 %collective-permute-done.2 = f32[2,256]{1,0:T(2,128)S(1)} collective-permute-done((f32[2,256]{1,0:T(2,128)S(1)}, f32[2,256]{1,0:T(2,128)S(1)}, u32[]{:S(2)}, u32[]{:S(2)}) %collective-permute-start.2) | collective-permute-done | bytes 2080 | tf_op jit(solution)/shard_map/ppermute | solution.py:453
  205.0 0.0 copy-done.11
  205.0 0.0 copy-done.12
  205.0 0.0 copy-done.13
  205.0 0.6 divide_subtract_fusion.1
  205.6 0.6 pad_maximum_fusion.1
  206.2 0.0 collective-permute-done.1
  206.2 0.0 copy-start.4
  206.2 2.0 copy-done.4
  208.2 0.0 copy-done.3
  208.2 0.0 copy-done.1
  208.2 9.3 %divide_subtract_fusion = (f32[256,4096]{1,0:T(8,128)}, f32[256,4096]{1,0:T(8,128)}, f32[256,4096]{1,0:T(8,128)}) fusion(f32[256,4096]{1,0:T(8,128)S(1)} %copy-done.1, f32[256,4096]{1,0:T(8,128)S(1)} %copy-done.3, f32[256,4096]{1,0:T(8,128)} %param.15, f32[256,4096]{1,0:T(8,128)} %copy-done.4, f32[256,4096]{1,0:T(8,128)S(1)} %fusion.24, ...), kind=kOutput, calls=%fused_computation.3 | convolution fusion | flops 821526528 | bytes 37487616 | tf_op jit(solution)/shard_map/dot_general | solution.py:22
  (4 shorter events, 0.0 us)
Async XLA Ops:
  1.3 42.1 %collective-permute-start = (bf16[2,256]{1,0:T(2,128)(2,1)S(1)}, bf16[2,256]{1,0:T(2,128)(2,1)S(1)}, u32[]{:S(2)}, u32[]{:S(2)}) collective-permute-start(bf16[2,256]{1,0:T(2,128)(2,1)S(1)} %convert_element_type.28), channel_id=1, source_target_pairs={{0,1},{1,0},{2,3},{3,2},{4,5},{5,4},{6,7},{7,6},{8,9},{9,8},{10,11... | collective-permute-start | bytes 3080 | tf_op jit(solution)/shard_map/ppermute | solution.py:431
  38.1 4.6 %copy-start.2 = (bf16[16,24,4096]{2,1,0:T(8,128)(2,1)S(1)}, bf16[16,24,4096]{2,1,0:T(8,128)(2,1)}, u32[]{:S(2)}) copy-start(bf16[16,24,4096]{2,1,0:T(8,128)(2,1)} %get-tuple-element.11) | copy-start | bytes 9437188
  126.0 64.4 %copy-start.8 = (bf16[384,256]{1,0:T(8,128)(2,1)S(1)}, bf16[384,256]{1,0:T(8,128)(2,1)}, u32[]{:S(2)}) copy-start(bf16[384,256]{1,0:T(8,128)(2,1)} %get-tuple-element.34.left_other) | copy-start | bytes 589828
  190.5 3.4 %copy-start = (bf16[384,4096]{1,0:T(8,128)(2,1)S(1)}, bf16[384,4096]{1,0:T(8,128)(2,1)}, u32[]{:S(2)}) copy-start(bf16[384,4096]{1,0:T(8,128)(2,1)} %shard_map.138) | copy-start | bytes 9437188
  190.5 3.5 %copy-start.6 = (bf16[256,4096]{1,0:T(8,128)(2,1)S(1)}, bf16[256,4096]{1,0:T(8,128)(2,1)}, u32[]{:S(2)}) copy-start(bf16[256,4096]{1,0:T(8,128)(2,1)} %get-tuple-element.13.weight_other) | copy-start | bytes 6291460
  190.5 3.5 %copy-start.10 = (f32[384,256]{1,0:T(8,128)S(1)}, f32[384,256]{1,0:T(8,128)}, u32[]{:S(2)}) copy-start(f32[384,256]{1,0:T(8,128)} %get-tuple-element.35) | copy-start | bytes 1179652
  195.2 3.1 %copy-start.5 = (bf16[256,4096]{1,0:T(8,128)(2,1)S(1)}, bf16[256,4096]{1,0:T(8,128)(2,1)}, u32[]{:S(2)}) copy-start(bf16[256,4096]{1,0:T(8,128)(2,1)} %get-tuple-element.12.weight_own) | copy-start | bytes 6291460
  195.2 3.1 %copy-start.9 = (f32[384,256]{1,0:T(8,128)S(1)}, f32[384,256]{1,0:T(8,128)}, u32[]{:S(2)}) copy-start(f32[384,256]{1,0:T(8,128)} %get-tuple-element.37) | copy-start | bytes 1179652
  196.7 2.7 %copy-start.7 = (bf16[384,256]{1,0:T(8,128)(2,1)S(1)}, bf16[384,256]{1,0:T(8,128)(2,1)}, u32[]{:S(2)}) copy-start(bf16[384,256]{1,0:T(8,128)(2,1)} %get-tuple-element.36.left_own) | copy-start | bytes 589828
  196.7 9.6 %collective-permute-start.1 = (f32[256,4096]{1,0:T(8,128)S(1)}, f32[256,4096]{1,0:T(8,128)S(1)}, u32[]{:S(2)}, u32[]{:S(2)}) collective-permute-start(f32[256,4096]{1,0:T(8,128)S(1)} %convolution_add_fusion), channel_id=1, source_target_pairs={{0,1},{1,0},{2,3},{3,2},{4,5},{5,4},{6,7},{7,6},{8,9},{9,8},{10,11... | collective-permute-start | bytes 12582920 | tf_op jit(solution)/shard_map/ppermute | solution.py:452
  198.3 6.8 %collective-permute-start.2 = (f32[2,256]{1,0:T(2,128)S(1)}, f32[2,256]{1,0:T(2,128)S(1)}, u32[]{:S(2)}, u32[]{:S(2)}) collective-permute-start(f32[2,256]{1,0:T(2,128)S(1)} %pad_maximum_fusion), channel_id=1, source_target_pairs={{0,1},{1,0},{2,3},{3,2},{4,5},{5,4},{6,7},{7,6},{8,9},{9,8},{10,11... | collective-permute-start | bytes 6152 | tf_op jit(solution)/shard_map/ppermute | solution.py:453
  198.3 9.9 %copy-start.3 = (f32[256,4096]{1,0:T(8,128)S(1)}, f32[256,4096]{1,0:T(8,128)}, u32[]{:S(2)}) copy-start(f32[256,4096]{1,0:T(8,128)} %param.14) | copy-start | bytes 12582916
  199.4 5.7 %copy-start.11 = (f32[2,256]{1,0:T(2,128)S(1)}, f32[2,256]{1,0:T(2,128)}, u32[]{:S(2)}) copy-start(f32[2,256]{1,0:T(2,128)} %param.13) | copy-start | bytes 6148
  199.4 5.6 %copy-start.12 = (f32[2,256]{1,0:T(2,128)S(1)}, f32[2,256]{1,0:T(2,128)}, u32[]{:S(2)}) copy-start(f32[2,256]{1,0:T(2,128)} %param.16) | copy-start | bytes 6148
  199.4 5.6 %copy-start.13 = (f32[2,256]{1,0:T(2,128)S(1)}, f32[2,256]{1,0:T(2,128)}, u32[]{:S(2)}) copy-start(f32[2,256]{1,0:T(2,128)} %param.17) | copy-start | bytes 6148
  199.4 8.8 %copy-start.1 = (f32[256,4096]{1,0:T(8,128)S(1)}, f32[256,4096]{1,0:T(8,128)}, u32[]{:S(2)}) copy-start(f32[256,4096]{1,0:T(8,128)} %weight_ref.1) | copy-start | bytes 12582916
  206.2 2.0 copy-start.4
